TPU v7x, 128 devices: a whole 4x4x4 slice. The times are simulated.
128 devices in a mesh: member: 16 (over z_lo, y, core), band: 8 (over x, z_hi).
Axes of the slice: x: 4, y: 4, z: 4 (z_hi: 2, z_lo: 2; z = z_hi * 2 + z_lo), core: 2. Of those that a mesh axis runs over, the one named last changes fastest.
Arguments:
- height_start: float32 [80, 512, 1024], P(None, 'member', 'band'), may hold values from -6 to 6
- east_start: float32 [80, 512, 1024], P(None, 'member', 'band'), may hold values from -6 to 6
- north_start: float32 [80, 512, 1024], P(None, 'member', 'band'), may hold values from -6 to 6
- obs_value: float32 [512, 1024], P('member', 'band'), may hold values from -8 to 8
- obs_mask: int32 [512, 1024], P('member', 'band'), may hold values 0 or 1
- obs_precision: float32 [512, 1024], P('member', 'band'), may hold values from 0.25 to 4
- step_sizes: int32 [2], replicated, may hold values from 4 to 12
Outputs:
- analysis_height: float32 [80, 512, 1024], P(None, 'member', 'band')
- analysis_east: float32 [80, 512, 1024], P(None, 'member', 'band')
- analysis_north: float32 [80, 512, 1024], P(None, 'member', 'band')
All inputs are finite; a program needn't handle non-finite values. No bound on the sum of `obs_mask` on one device may be relied on, other than what follows from the above.
Results may differ from a plain program's by a relative error of at most 0.0001.
Values sent between devices are 32-bit elements; how exact they have to be, the bound alone decides.
A program may use at most 128 MiB of HBM per device.

v0:
```python
import jax
import jax.numpy as jnp
from jax import lax
from jax.sharding import Mesh
from jax.sharding import PartitionSpec as P

STEPS = 3
ITERS = 2
LWIDTH = 32
LSCALE = 12
MEMBER = ("member_0", "member_1", "member_2")
BAND = ("band_0", "band_1")
MEMBER_BAND = ("member_0", "member_1", "member_2", "band_0", "band_1")


highest = lax.Precision.HIGHEST


def extended(block, sides, width, periodic):
    for axis, dim in sides:
        count = lax.axis_size(axis)
        forward = [(i, i + 1) for i in range(count - 1)]
        if periodic:
            forward.append((count - 1, 0))
        backward = [(target, source) for source, target in forward]
        low = lax.ppermute(
            lax.slice_in_dim(block, block.shape[dim] - width, None, axis=dim), axis, forward
        )
        high = lax.ppermute(lax.slice_in_dim(block, 0, width, axis=dim), axis, backward)
        block = jnp.concatenate([low, block, high], axis=dim)
    return block


def one_axis_at_a_time(array, axes):
    for axis in axes:
        array = lax.psum(array, axis)
    return array


def taper_kernel(outputs, inputs, margin, spread):
    out_index = jnp.arange(outputs, dtype=jnp.int32)[:, None]
    in_index = jnp.arange(inputs, dtype=jnp.int32)[None, :]
    offset = (in_index - margin - out_index).astype(jnp.float32)
    scaled_off = offset / spread
    weight = jnp.exp(-0.5 * scaled_off * scaled_off)
    return jnp.where(jnp.abs(offset) <= margin, weight, jnp.zeros_like(weight))


def taper_rows(padded, row_count, margin, spread):
    kernel = taper_kernel(row_count, row_count + 2 * margin, margin, spread)
    return jnp.einsum("ab,mbc->mac", kernel, padded, precision=highest)


def taper_columns(padded, columns, margin, spread):
    block_size = 128
    windows = jnp.stack([padded], axis=2)
    kernel = taper_kernel(block_size, block_size + 2 * margin, margin, spread)
    result = jnp.einsum("mrjk,bk->mrjb", windows, kernel, precision=highest)
    return result.reshape(padded.shape[0], padded.shape[1], columns)


def wave_edges(stacked, margin):
    rows_done = extended(stacked, ((MEMBER, 2),), margin, False)
    return extended(rows_done, ((BAND, 3),), margin, True)


def advance_deep(height, eastward, northward, valid_rows):
    padded = wave_edges(jnp.stack([height, eastward, northward]), 2)
    height_pad = padded[0]
    east_pad = padded[1]
    north_pad = padded[2]
    wide_height = height_pad[:, 1:-1, 1:-1] - 0.2 * (
        east_pad[:, 1:-1, 2:]
        - east_pad[:, 1:-1, :-2]
        + (north_pad[:, 2:, 1:-1] - north_pad[:, :-2, 1:-1])
    )
    wide_height = jnp.where(valid_rows[None, :, None], wide_height, jnp.zeros_like(wide_height))
    new_height = wide_height[:, 1:-1, 1:-1]
    new_east = (
        eastward + 0.1 * northward - 0.2 * (wide_height[:, 1:-1, 2:] - wide_height[:, 1:-1, :-2])
    )
    new_north = (
        northward - 0.1 * eastward - 0.2 * (wide_height[:, 2:, 1:-1] - wide_height[:, :-2, 1:-1])
    )
    return (new_height, new_east, new_north)


def descend(anomalies, member_means, observed, step_sizes, cell_total, gather_state, localize):
    weights = jnp.zeros_like(anomalies[0])
    for iteration in range(ITERS):
        if iteration == 0:
            analysis_state = member_means
        else:
            analysis_state = member_means + gather_state(jnp.sum(anomalies * weights[None], axis=1))
        residual = observed[1] * (
            observed[0]
            - analysis_state[0]
            - 0.15 * (analysis_state[1] * analysis_state[1] + analysis_state[2] * analysis_state[2])
        )
        contrib = (
            anomalies[0]
            + 0.3 * (analysis_state[1] * anomalies[1] + analysis_state[2] * anomalies[2])
        ) * residual
        gradient = weights - localize(contrib)
        square_total = one_axis_at_a_time(jnp.sum(gradient * gradient), MEMBER_BAND)
        factor = (
            step_sizes[iteration].astype(jnp.float32)
            / 64.0
            / jnp.sqrt(square_total / cell_total + 1e-06)
        )
        weights = weights - factor * gradient
    return weights


def analyse_tiles(ensemble, observed, step_sizes, cell_total, root_scale, members):
    member_means = jnp.sum(ensemble, axis=1) / members
    anomalies = (ensemble - member_means[:, None]) / root_scale

    def local_state(partial_sum):
        return partial_sum

    def localize(contrib):
        padded = extended(contrib, ((MEMBER, 1),), LWIDTH, False)
        lat_done = taper_rows(padded, contrib.shape[1], LWIDTH, LSCALE)
        wrapped = extended(lat_done, ((BAND, 2),), LWIDTH, True)
        return taper_columns(wrapped, contrib.shape[2], LWIDTH, LSCALE)

    weights = descend(
        anomalies, member_means, observed, step_sizes, cell_total, local_state, localize
    )
    return jnp.sum(anomalies * weights[None], axis=1)


def per_device(
    height_start, east_start, north_start, obs_value, obs_mask, obs_precision, step_sizes
):
    members = height_start.shape[0]
    row_count = height_start.shape[1]
    col_count = height_start.shape[2]
    height, eastward, northward = (height_start, east_start, north_start)
    global_rows = (
        lax.axis_index(MEMBER) * row_count - 1 + jnp.arange(row_count + 2, dtype=jnp.int32)
    )
    valid_rows = (global_rows >= 0) & (global_rows < row_count * lax.axis_size(MEMBER))
    for section_number in range(STEPS):
        height, eastward, northward = advance_deep(height, eastward, northward, valid_rows)
    ensemble = jnp.stack([height, eastward, northward])
    obs_weight = obs_mask.astype(jnp.float32) * obs_precision
    observed = jnp.stack([obs_value, obs_weight])
    cell_total = float(
        members * row_count * col_count * lax.axis_size(MEMBER) * lax.axis_size(BAND)
    )
    root_scale = jnp.sqrt(jnp.float32(members - 1))
    increment = analyse_tiles(ensemble, observed, step_sizes, cell_total, root_scale, members)
    analysis = ensemble + increment[:, None]
    return (analysis[0], analysis[1], analysis[2])


def solution(mesh):
    torus = Mesh(
        mesh.devices.reshape(2, 4, 2, 4, 2),
        ("member_0", "member_1", "member_2", "band_0", "band_1"),
    )
    in_specs = (
        P(None, MEMBER, BAND),
        P(None, MEMBER, BAND),
        P(None, MEMBER, BAND),
        P(MEMBER, BAND),
        P(MEMBER, BAND),
        P(MEMBER, BAND),
        P(),
    )
    out_specs = (P(None, MEMBER, BAND), P(None, MEMBER, BAND), P(None, MEMBER, BAND))
    return jax.shard_map(
        per_device, mesh=torus, in_specs=in_specs, out_specs=out_specs, check_vma=False
    )
```

profile of v0, /device:TPU:0, one launch (start us, length us, event | category | flops | bytes accessed | tf_op | source)
XLA Modules:
  0.0 400.6 jit_solution(12849979625109068279)
XLA Ops:
  5.8 4.0 collective-permute-done.1
  11.8 5.3 %fusion.117 = (f32[3,80,36,2]{3,2,1,0:T(8,128)}, f32[3,80,36,2]{3,2,1,0:T(8,128)}) fusion(f32[3,80,36,128]{3,2,1,0:T(8,128)S(1)} %pad_maximum_fusion.3), kind=kLoop, calls=%fused_computation.180 | loop fusion | bytes 276480 | tf_op jit(solution)/shard_map/slice | solution.py:27
  17.2 3.8 copy.10
  21.0 3.9 collective-permute-start.2
  38.9 10.7 %pad_maximum_fusion = f32[3,80,36,132]{3,2,1,0:T(8,128)S(1)} fusion(f32[3,80,36,2]{3,2,1,0:T(8,128)} %copy.13, f32[3,80,2,128]{3,2,1,0:T(2,128)S(1)} %collective-permute-done.1, f32[1,80,32,128]{3,2,1,0:T(8,128)S(1)} %bitcast.125, f32[1,80,32,128]{3,2,1,0:T(8,128)S(1)} %bitcast.128, f32[1,80,32,128]{3,2,1,0:T(8,128)} %bitcast.131, ...), kind=kLoop, calls=%fused_computation | loop fusion | flops 6842880 | bytes 9123840 | tf_op jit(solution)/shard_map/concatenate | solution.py:30
  51.9 5.8 %fusion.23 = f32[80,34,130]{2,1,0:T(8,128)S(1)} fusion(f32[80,36,132]{2,1,0:T(8,128)S(1)} %get-tuple-element.10, f32[80,36,132]{2,1,0:T(8,128)S(1)} %get-tuple-element.11, f32[80,36,132]{2,1,0:T(8,128)} %get-tuple-element.9, pred[34]{0:T(512)(128)(4,1)S(1)} %copy-done.24), kind=kLoop, calls=%fused_computation.44 | loop fusion | flops 2121600 | bytes 8486434 | tf_op jit(solution)/shard_map/jit(_where)/select_n | solution.py:77
  59.5 6.2 %collective-permute-start.4 = (f32[3,80,2,128]{3,2,1,0:T(2,128)S(1)}, f32[3,80,2,128]{3,2,1,0:T(2,128)S(1)}, u32[]{:S(2)}, u32[]{:S(2)}) collective-permute-start(f32[3,80,2,128]{3,2,1,0:T(2,128)S(1)} %get-tuple-element.29), channel_id=1, source_target_pairs={{0,8},{8,16},{16,24},{24,32},{32,40},{40,48},{48,56},{56,64},{64,7... | collective-permute-start | bytes 737288 | tf_op jit(solution)/shard_map/ppermute | solution.py:26
  70.2 5.3 %fusion.116 = (f32[3,80,36,2]{3,2,1,0:T(8,128)}, f32[3,80,36,2]{3,2,1,0:T(8,128)}) fusion(f32[3,80,36,128]{3,2,1,0:T(8,128)S(1)} %pad_maximum_fusion.4), kind=kLoop, calls=%fused_computation.179 | loop fusion | bytes 276480 | tf_op jit(solution)/shard_map/slice | solution.py:27
  75.5 3.8 copy.14
  84.7 4.2 %collective-permute-start.7 = (f32[3,80,36,2]{1,3,2,0:T(2,128)S(1)}, f32[3,80,36,2]{1,3,2,0:T(2,128)S(1)}, u32[]{:S(2)}, u32[]{:S(2)}) collective-permute-start(f32[3,80,36,2]{1,3,2,0:T(2,128)S(1)} %copy.15), channel_id=1, source_target_pairs={{1,0},{2,1},{3,2},{4,3},{5,4},{6,5},{7,6},{0,7},{9,8},{10,9},{11,1... | collective-permute-start | bytes 207368 | tf_op jit(solution)/shard_map/ppermute | solution.py:29
  96.0 10.7 %pad_maximum_fusion.1 = f32[3,80,36,132]{3,2,1,0:T(8,128)S(1)} fusion(f32[3,80,36,2]{3,2,1,0:T(8,128)} %copy.17, f32[3,80,2,128]{3,2,1,0:T(2,128)S(1)} %collective-permute-done.5, f32[1,80,32,128]{3,2,1,0:T(8,128)S(1)} %bitcast.122, f32[1,80,32,128]{3,2,1,0:T(8,128)S(1)} %bitcast.119, f32[1,80,32,128]{3,2,1,0:T(8,128)} %copy-done.18, ...), kind=kLoop, calls=%fused_computation.1 | loop fusion | flops 6842880 | bytes 9123840 | tf_op jit(solution)/shard_map/concatenate | solution.py:30
  109.1 5.8 %fusion.19 = f32[80,34,130]{2,1,0:T(8,128)S(1)} fusion(f32[80,36,132]{2,1,0:T(8,128)S(1)} %get-tuple-element.7, f32[80,36,132]{2,1,0:T(8,128)S(1)} %get-tuple-element.8, f32[80,36,132]{2,1,0:T(8,128)} %get-tuple-element.6, pred[34]{0:T(512)(128)(4,1)S(1)} %copy-done.25), kind=kLoop, calls=%fused_computation.35 | loop fusion | flops 2121600 | bytes 8486434 | tf_op jit(solution)/shard_map/jit(_where)/select_n | solution.py:77
  116.6 6.0 %collective-permute-start.8 = (f32[3,80,2,128]{3,2,1,0:T(2,128)S(1)}, f32[3,80,2,128]{3,2,1,0:T(2,128)S(1)}, u32[]{:S(2)}, u32[]{:S(2)}) collective-permute-start(f32[3,80,2,128]{3,2,1,0:T(2,128)S(1)} %get-tuple-element.27), channel_id=1, source_target_pairs={{0,8},{8,16},{16,24},{24,32},{32,40},{40,48},{48,56},{56,64},{64,7... | collective-permute-start | bytes 737288 | tf_op jit(solution)/shard_map/ppermute | solution.py:26
  126.9 5.3 %fusion.115 = (f32[3,80,36,2]{3,2,1,0:T(8,128)}, f32[3,80,36,2]{3,2,1,0:T(8,128)}) fusion(f32[3,80,36,128]{3,2,1,0:T(8,128)S(1)} %pad_maximum_fusion.5), kind=kLoop, calls=%fused_computation.178 | loop fusion | bytes 276480 | tf_op jit(solution)/shard_map/slice | solution.py:27
  132.2 3.8 copy.18
  152.7 10.7 %pad_maximum_fusion.2 = f32[3,80,36,132]{3,2,1,0:T(8,128)S(1)} fusion(f32[3,80,36,2]{3,2,1,0:T(8,128)} %copy.21, f32[3,80,2,128]{3,2,1,0:T(2,128)S(1)} %collective-permute-done.9, f32[1,80,32,128]{3,2,1,0:T(8,128)S(1)} %bitcast.116, f32[1,80,32,128]{3,2,1,0:T(8,128)S(1)} %bitcast.113, f32[1,80,32,128]{3,2,1,0:T(8,128)} %copy-done.17, ...), kind=kLoop, calls=%fused_computation.2 | loop fusion | flops 6842880 | bytes 9123840 | tf_op jit(solution)/shard_map/concatenate | solution.py:30
  165.8 5.6 %fusion.15 = f32[80,34,130]{2,1,0:T(8,128)S(1)} fusion(f32[80,36,132]{2,1,0:T(8,128)S(1)} %get-tuple-element.4, f32[80,36,132]{2,1,0:T(8,128)S(1)} %get-tuple-element.5, f32[80,36,132]{2,1,0:T(8,128)} %get-tuple-element.3, pred[34]{0:T(512)(128)(4,1)S(1)} %copy-done.26), kind=kLoop, calls=%fused_computation.26 | loop fusion | flops 2121600 | bytes 8486434 | tf_op jit(solution)/shard_map/jit(_where)/select_n | solution.py:77
  175.9 5.9 %collective-permute-start.12 = (f32[80,32,128]{2,1,0:T(8,128)S(1)}, f32[80,32,128]{2,1,0:T(8,128)S(1)}, u32[]{:S(2)}, u32[]{:S(2)}) collective-permute-start(f32[80,32,128]{2,1,0:T(8,128)S(1)} %add_multiply_fusion.1), channel_id=1, source_target_pairs={{0,8},{8,16},{16,24},{24,32},{32,40},{40,48},{48,56},{56,64},{64,7... | collective-permute-start | bytes 3932168 | tf_op jit(solution)/shard_map/ppermute | solution.py:26
  198.1 4.6 %collective-permute-start.15 = (f32[80,32,32]{0,2,1:T(8,128)}, f32[80,32,32]{0,2,1:T(8,128)}, u32[]{:S(2)}, u32[]{:S(2)}) collective-permute-start(f32[80,32,32]{0,2,1:T(8,128)} %copy.23), channel_id=1, source_target_pairs={{1,0},{2,1},{3,2},{4,3},{5,4},{6,5},{7,6},{0,7},{9,8},{10,9},{11,1... | collective-permute-start | bytes 983048 | tf_op jit(solution)/shard_map/ppermute | solution.py:29
  202.6 24.1 %collective-permute-done.14 = f32[80,32,32]{0,2,1:T(8,128)} collective-permute-done((f32[80,32,32]{0,2,1:T(8,128)S(1)}, f32[80,32,32]{0,2,1:T(8,128)}, u32[]{:S(2)}, u32[]{:S(2)}) %collective-permute-start.14) | collective-permute-done | bytes 327712 | tf_op jit(solution)/shard_map/ppermute | solution.py:26
  232.8 6.4 %multiply_reduce_fusion.3 = (f32[]{:T(128)}, f32[80,32,128]{2,1,0:T(8,128)}) fusion(s32[192]{0:T(256)S(1)} %iota_add_fusion, f32[80,32,32]{2,1,0:T(8,128)} %copy.25, f32[80,32,128]{2,1,0:T(8,128)} %copy-done.20, f32[80,32,32]{2,1,0:T(8,128)} %copy.24), kind=kOutput, calls=%fused_computation.99 | convolution fusion | flops 757137408 | bytes 3277572 | tf_op jit(solution)/shard_map/mrjk,bk->mrjb/dot_general | solution.py:58
  239.3 14.1 %psum.70 = f32[]{:T(128)} all-reduce(f32[]{:T(128)} %get-tuple-element.46), channel_id=1, replica_groups=mesh['member_0'=2,'member_1'=4,'member_2'=2,'band_0'=4,'band_1'=2] {'mem..., use_global_device_ids=true, to_apply=%region_2.3 | all-reduce | flops 1 | bytes 8 | tf_op jit(solution)/shard_map/psum | solution.py:36
  253.4 9.0 %psum.71 = f32[]{:T(128)} all-reduce(f32[]{:T(128)} %psum.70), channel_id=1, replica_groups=mesh['member_0'=2,'member_1'=4,'member_2'=2,'band_0'=4,'band_1'=2] {'mem..., use_global_device_ids=true, to_apply=%region_3.4 | all-reduce | flops 1 | bytes 8 | tf_op jit(solution)/shard_map/psum | solution.py:36
  262.9 5.2 %psum.72 = f32[]{:T(128)} all-reduce(f32[]{:T(128)} %psum.71), channel_id=1, replica_groups=mesh['member_0'=2,'member_1'=4,'member_2'=2,'band_0'=4,'band_1'=2] {'mem..., use_global_device_ids=true, to_apply=%region_4.5 | all-reduce | flops 1 | bytes 8 | tf_op jit(solution)/shard_map/psum | solution.py:36
  268.8 11.4 %psum.73 = f32[]{:T(128)} all-reduce(f32[]{:T(128)} %psum.72), channel_id=1, replica_groups=mesh['member_0'=2,'member_1'=4,'member_2'=2,'band_0'=4,'band_1'=2] {'ban..., use_global_device_ids=true, to_apply=%region_5.6 | all-reduce | flops 1 | bytes 8 | tf_op jit(solution)/shard_map/psum | solution.py:36
  280.2 7.3 %psum.74 = f32[]{:T(128)} all-reduce(f32[]{:T(128)} %psum.73), channel_id=1, replica_groups=mesh['member_0'=2,'member_1'=4,'member_2'=2,'band_0'=4,'band_1'=2] {'ban..., use_global_device_ids=true, to_apply=%region_6.7 | all-reduce | flops 1 | bytes 8 | tf_op jit(solution)/shard_map/psum | solution.py:36
  315.0 7.4 %collective-permute-done.18 = f32[80,32,32]{0,2,1:T(8,128)} collective-permute-done((f32[80,32,32]{0,2,1:T(8,128)S(1)}, f32[80,32,32]{0,2,1:T(8,128)}, u32[]{:S(2)}, u32[]{:S(2)}) %collective-permute-start.18) | collective-permute-done | bytes 327712 | tf_op jit(solution)/shard_map/ppermute | solution.py:26
  329.7 6.8 %multiply_reduce_fusion.2 = (f32[]{:T(128)}, f32[80,32,128]{2,1,0:T(8,128)}) fusion(s32[192]{0:T(256)S(1)} %iota_add_fusion, f32[80,32,32]{2,1,0:T(8,128)} %copy.29, f32[80,32,128]{2,1,0:T(8,128)} %copy-done.19, f32[80,32,32]{2,1,0:T(8,128)} %copy.28, f32[80,32,128]{2,1,0:T(8,128)} %get-tuple-element.47, f32[]{:T(128)S(6)} %div.55), kind=kOutput, calls=%fused_computation.96 | convolution fusion | flops 757792768 | bytes 4588296 | tf_op jit(solution)/shard_map/mrjk,bk->mrjb/dot_general | solution.py:58
  336.5 28.5 %psum.75 = f32[]{:T(128)} all-reduce(f32[]{:T(128)} %get-tuple-element.48), channel_id=1, replica_groups=mesh['member_0'=2,'member_1'=4,'member_2'=2,'band_0'=4,'band_1'=2] {'mem..., use_global_device_ids=true, to_apply=%region_9.10 | all-reduce | flops 1 | bytes 8 | tf_op jit(solution)/shard_map/psum | solution.py:36
  365.0 9.6 %psum.76 = f32[]{:T(128)} all-reduce(f32[]{:T(128)} %psum.75), channel_id=1, replica_groups=mesh['member_0'=2,'member_1'=4,'member_2'=2,'band_0'=4,'band_1'=2] {'mem..., use_global_device_ids=true, to_apply=%region_10.11 | all-reduce | flops 1 | bytes 8 | tf_op jit(solution)/shard_map/psum | solution.py:36
  378.3 8.4 %psum.78 = f32[]{:T(128)} all-reduce(f32[]{:T(128)} %psum.77), channel_id=1, replica_groups=mesh['member_0'=2,'member_1'=4,'member_2'=2,'band_0'=4,'band_1'=2] {'ban..., use_global_device_ids=true, to_apply=%region_12.13 | all-reduce | flops 1 | bytes 8 | tf_op jit(solution)/shard_map/psum | solution.py:36
  386.7 7.6 %psum.79 = f32[]{:T(128)} all-reduce(f32[]{:T(128)} %psum.78), channel_id=1, replica_groups=mesh['member_0'=2,'member_1'=4,'member_2'=2,'band_0'=4,'band_1'=2] {'ban..., use_global_device_ids=true, to_apply=%region_13.14 | all-reduce | flops 1 | bytes 8 | tf_op jit(solution)/shard_map/psum | solution.py:36
  (141 shorter events, 139.0 us)
Async XLA Ops:
  0.6 9.1 %copy-start.15 = (f32[80,32,128]{2,1,0:T(8,128)S(1)}, f32[80,32,128]{2,1,0:T(8,128)}, u32[]{:S(2)}) copy-start(f32[80,32,128]{2,1,0:T(8,128)} %param.8) | copy-start | bytes 3932164
  0.6 9.1 %copy-start.13 = (f32[80,32,128]{2,1,0:T(8,128)S(1)}, f32[80,32,128]{2,1,0:T(8,128)}, u32[]{:S(2)}) copy-start(f32[80,32,128]{2,1,0:T(8,128)} %param.9) | copy-start | bytes 3932164
  3.2 2.6 collective-permute-start
  4.5 5.3 %collective-permute-start.1 = (f32[3,80,2,128]{3,2,1,0:T(2,128)S(1)}, f32[3,80,2,128]{3,2,1,0:T(2,128)S(1)}, u32[]{:S(2)}, u32[]{:S(2)}) collective-permute-start(f32[3,80,2,128]{3,2,1,0:T(2,128)S(1)} %get-tuple-element.32), channel_id=1, source_target_pairs={{8,0},{16,8},{24,16},{32,24},{40,32},{48,40},{56,48},{64,56},{72,6... | collective-permute-start | bytes 737288 | tf_op jit(solution)/shard_map/ppermute | solution.py:29
  21.0 10.8 %collective-permute-start.2 = (f32[3,80,36,2]{1,3,2,0:T(2,128)S(1)}, f32[3,80,36,2]{1,3,2,0:T(2,128)S(1)}, u32[]{:S(2)}, u32[]{:S(2)}) collective-permute-start(f32[3,80,36,2]{1,3,2,0:T(2,128)S(1)} %copy.10), channel_id=1, source_target_pairs={{0,1},{1,2},{2,3},{3,4},{4,5},{5,6},{6,7},{7,0},{8,9},{9,10},{10,1... | collective-permute-start | bytes 207368 | tf_op jit(solution)/shard_map/ppermute | solution.py:26
  28.8 6.6 %collective-permute-start.3 = (f32[3,80,36,2]{1,3,2,0:T(2,128)S(1)}, f32[3,80,36,2]{1,3,2,0:T(2,128)S(1)}, u32[]{:S(2)}, u32[]{:S(2)}) collective-permute-start(f32[3,80,36,2]{1,3,2,0:T(2,128)S(1)} %copy.11), channel_id=1, source_target_pairs={{1,0},{2,1},{3,2},{4,3},{5,4},{6,5},{7,6},{0,7},{9,8},{10,9},{11,1... | collective-permute-start | bytes 207368 | tf_op jit(solution)/shard_map/ppermute | solution.py:29
  51.9 5.9 %copy-start.14 = (f32[80,32,128]{2,1,0:T(8,128)S(1)}, f32[80,32,128]{2,1,0:T(8,128)}, u32[]{:S(2)}) copy-start(f32[80,32,128]{2,1,0:T(8,128)} %param.9) | copy-start | bytes 3932164
  51.9 5.9 %copy-start.16 = (f32[80,32,128]{2,1,0:T(8,128)S(1)}, f32[80,32,128]{2,1,0:T(8,128)}, u32[]{:S(2)}) copy-start(f32[80,32,128]{2,1,0:T(8,128)} %param.8) | copy-start | bytes 3932164
  59.2 16.3 %copy-start.18 = (f32[1,80,32,128]{3,2,1,0:T(8,128)}, f32[1,80,32,128]{3,2,1,0:T(8,128)S(1)}, u32[]{:S(2)}) copy-start(f32[1,80,32,128]{3,2,1,0:T(8,128)S(1)} %get-tuple-element.35) | copy-start | bytes 3932164
  59.2 36.8 %copy-start.9 = (f32[80,32,128]{2,1,0:T(8,128)}, f32[80,32,128]{2,1,0:T(8,128)S(1)}, u32[]{:S(2)}) copy-start(f32[80,32,128]{2,1,0:T(8,128)S(1)} %get-tuple-element.16) | copy-start | bytes 3932164
  59.2 36.8 %copy-start.11 = (f32[80,32,128]{2,1,0:T(8,128)}, f32[80,32,128]{2,1,0:T(8,128)S(1)}, u32[]{:S(2)}) copy-start(f32[80,32,128]{2,1,0:T(8,128)S(1)} %get-tuple-element.17) | copy-start | bytes 3932164
  59.5 8.0 %collective-permute-start.4 = (f32[3,80,2,128]{3,2,1,0:T(2,128)S(1)}, f32[3,80,2,128]{3,2,1,0:T(2,128)S(1)}, u32[]{:S(2)}, u32[]{:S(2)}) collective-permute-start(f32[3,80,2,128]{3,2,1,0:T(2,128)S(1)} %get-tuple-element.29), channel_id=1, source_target_pairs={{0,8},{8,16},{16,24},{24,32},{32,40},{40,48},{48,56},{56,64},{64,7... | collective-permute-start | bytes 737288 | tf_op jit(solution)/shard_map/ppermute | solution.py:26
  65.7 3.5 collective-permute-start.5
  79.3 9.6 %collective-permute-start.6 = (f32[3,80,36,2]{1,3,2,0:T(2,128)S(1)}, f32[3,80,36,2]{1,3,2,0:T(2,128)S(1)}, u32[]{:S(2)}, u32[]{:S(2)}) collective-permute-start(f32[3,80,36,2]{1,3,2,0:T(2,128)S(1)} %copy.14), channel_id=1, source_target_pairs={{0,1},{1,2},{2,3},{3,4},{4,5},{5,6},{6,7},{7,0},{8,9},{9,10},{10,1... | collective-permute-start | bytes 207368 | tf_op jit(solution)/shard_map/ppermute | solution.py:26
  84.7 7.8 %collective-permute-start.7 = (f32[3,80,36,2]{1,3,2,0:T(2,128)S(1)}, f32[3,80,36,2]{1,3,2,0:T(2,128)S(1)}, u32[]{:S(2)}, u32[]{:S(2)}) collective-permute-start(f32[3,80,36,2]{1,3,2,0:T(2,128)S(1)} %copy.15), channel_id=1, source_target_pairs={{1,0},{2,1},{3,2},{4,3},{5,4},{6,5},{7,6},{0,7},{9,8},{10,9},{11,1... | collective-permute-start | bytes 207368 | tf_op jit(solution)/shard_map/ppermute | solution.py:29
  109.1 5.9 %copy-start.12 = (f32[80,32,128]{2,1,0:T(8,128)S(1)}, f32[80,32,128]{2,1,0:T(8,128)}, u32[]{:S(2)}) copy-start(f32[80,32,128]{2,1,0:T(8,128)} %copy-done.11) | copy-start | bytes 3932164
  116.4 15.9 %copy-start.17 = (f32[1,80,32,128]{3,2,1,0:T(8,128)}, f32[1,80,32,128]{3,2,1,0:T(8,128)S(1)}, u32[]{:S(2)}) copy-start(f32[1,80,32,128]{3,2,1,0:T(8,128)S(1)} %get-tuple-element.34) | copy-start | bytes 3932164
  116.4 36.4 %copy-start.5 = (f32[80,32,128]{2,1,0:T(8,128)}, f32[80,32,128]{2,1,0:T(8,128)S(1)}, u32[]{:S(2)}) copy-start(f32[80,32,128]{2,1,0:T(8,128)S(1)} %get-tuple-element.14) | copy-start | bytes 3932164
  116.4 36.4 %copy-start.7 = (f32[80,32,128]{2,1,0:T(8,128)}, f32[80,32,128]{2,1,0:T(8,128)S(1)}, u32[]{:S(2)}) copy-start(f32[80,32,128]{2,1,0:T(8,128)S(1)} %get-tuple-element.15) | copy-start | bytes 3932164
  116.6 7.5 %collective-permute-start.8 = (f32[3,80,2,128]{3,2,1,0:T(2,128)S(1)}, f32[3,80,2,128]{3,2,1,0:T(2,128)S(1)}, u32[]{:S(2)}, u32[]{:S(2)}) collective-permute-start(f32[3,80,2,128]{3,2,1,0:T(2,128)S(1)} %get-tuple-element.27), channel_id=1, source_target_pairs={{0,8},{8,16},{16,24},{24,32},{32,40},{40,48},{48,56},{56,64},{64,7... | collective-permute-start | bytes 737288 | tf_op jit(solution)/shard_map/ppermute | solution.py:26
  122.6 3.4 collective-permute-start.9
  136.1 9.6 %collective-permute-start.10 = (f32[3,80,36,2]{1,3,2,0:T(2,128)S(1)}, f32[3,80,36,2]{1,3,2,0:T(2,128)S(1)}, u32[]{:S(2)}, u32[]{:S(2)}) collective-permute-start(f32[3,80,36,2]{1,3,2,0:T(2,128)S(1)} %copy.18), channel_id=1, source_target_pairs={{0,1},{1,2},{2,3},{3,4},{4,5},{5,6},{6,7},{7,0},{8,9},{9,10},{10,1... | collective-permute-start | bytes 207368 | tf_op jit(solution)/shard_map/ppermute | solution.py:26
  142.6 6.6 %collective-permute-start.11 = (f32[3,80,36,2]{1,3,2,0:T(2,128)S(1)}, f32[3,80,36,2]{1,3,2,0:T(2,128)S(1)}, u32[]{:S(2)}, u32[]{:S(2)}) collective-permute-start(f32[3,80,36,2]{1,3,2,0:T(2,128)S(1)} %copy.19), channel_id=1, source_target_pairs={{1,0},{2,1},{3,2},{4,3},{5,4},{6,5},{7,6},{0,7},{9,8},{10,9},{11,1... | collective-permute-start | bytes 207368 | tf_op jit(solution)/shard_map/ppermute | solution.py:29
  175.9 8.5 %collective-permute-start.12 = (f32[80,32,128]{2,1,0:T(8,128)S(1)}, f32[80,32,128]{2,1,0:T(8,128)S(1)}, u32[]{:S(2)}, u32[]{:S(2)}) collective-permute-start(f32[80,32,128]{2,1,0:T(8,128)S(1)} %add_multiply_fusion.1), channel_id=1, source_target_pairs={{0,8},{8,16},{16,24},{24,32},{32,40},{40,48},{48,56},{56,64},{64,7... | collective-permute-start | bytes 3932168 | tf_op jit(solution)/shard_map/ppermute | solution.py:26
  181.9 4.9 %collective-permute-start.13 = (f32[80,32,128]{2,1,0:T(8,128)S(1)}, f32[80,32,128]{2,1,0:T(8,128)S(1)}, u32[]{:S(2)}, u32[]{:S(2)}) collective-permute-start(f32[80,32,128]{2,1,0:T(8,128)S(1)} %add_multiply_fusion.1), channel_id=1, source_target_pairs={{8,0},{16,8},{24,16},{32,24},{40,32},{48,40},{56,48},{64,56},{72,6... | collective-permute-start | bytes 3932168 | tf_op jit(solution)/shard_map/ppermute | solution.py:29
  194.1 32.6 %collective-permute-start.14 = (f32[80,32,32]{0,2,1:T(8,128)S(1)}, f32[80,32,32]{0,2,1:T(8,128)}, u32[]{:S(2)}, u32[]{:S(2)}) collective-permute-start(f32[80,32,32]{0,2,1:T(8,128)S(1)} %copy.22), channel_id=1, source_target_pairs={{0,1},{1,2},{2,3},{3,4},{4,5},{5,6},{6,7},{7,0},{8,9},{9,10},{10,1... | collective-permute-start | bytes 983048 | tf_op jit(solution)/shard_map/ppermute | solution.py:26
  198.1 31.7 %collective-permute-start.15 = (f32[80,32,32]{0,2,1:T(8,128)}, f32[80,32,32]{0,2,1:T(8,128)}, u32[]{:S(2)}, u32[]{:S(2)}) collective-permute-start(f32[80,32,32]{0,2,1:T(8,128)} %copy.23), channel_id=1, source_target_pairs={{1,0},{2,1},{3,2},{4,3},{5,4},{6,5},{7,6},{0,7},{9,8},{10,9},{11,1... | collective-permute-start | bytes 983048 | tf_op jit(solution)/shard_map/ppermute | solution.py:29
  232.8 29.5 %copy-start.27 = (s32[2]{0:T(128)S(1)}, s32[2]{0:T(128)}, u32[]{:S(2)}) copy-start(s32[2]{0:T(128)} %param.13) | copy-start | bytes 28
  292.5 3.9 collective-permute-start.16
  293.9 5.3 %collective-permute-start.17 = (f32[80,32,128]{2,1,0:T(8,128)S(1)}, f32[80,32,128]{2,1,0:T(8,128)S(1)}, u32[]{:S(2)}, u32[]{:S(2)}) collective-permute-start(f32[80,32,128]{2,1,0:T(8,128)S(1)} %add_multiply_fusion), channel_id=1, source_target_pairs={{8,0},{16,8},{24,16},{32,24},{40,32},{48,40},{56,48},{64,56},{72,6... | collective-permute-start | bytes 3932168 | tf_op jit(solution)/shard_map/ppermute | solution.py:29
  306.5 15.9 %collective-permute-start.18 = (f32[80,32,32]{0,2,1:T(8,128)S(1)}, f32[80,32,32]{0,2,1:T(8,128)}, u32[]{:S(2)}, u32[]{:S(2)}) collective-permute-start(f32[80,32,32]{0,2,1:T(8,128)S(1)} %copy.26), channel_id=1, source_target_pairs={{0,1},{1,2},{2,3},{3,4},{4,5},{5,6},{6,7},{7,0},{8,9},{9,10},{10,1... | collective-permute-start | bytes 983048 | tf_op jit(solution)/shard_map/ppermute | solution.py:26
  312.9 13.8 %collective-permute-start.19 = (f32[80,32,32]{0,2,1:T(8,128)}, f32[80,32,32]{0,2,1:T(8,128)}, u32[]{:S(2)}, u32[]{:S(2)}) collective-permute-start(f32[80,32,32]{0,2,1:T(8,128)} %copy.27), channel_id=1, source_target_pairs={{1,0},{2,1},{3,2},{4,3},{5,4},{6,5},{7,6},{0,7},{9,8},{10,9},{11,1... | collective-permute-start | bytes 983048 | tf_op jit(solution)/shard_map/ppermute | solution.py:29
  (16 other events, 37.9 us)
where the time goes:
time: 406 us; the launch traced here: 401 us
  blocking collectives  104 us (26%)
  local copies, waits for them, and re-layouts  101 us (25%)
  other arithmetic  68.6 us (17%)
  starting transfers between devices  57.7 us (14%)
  waiting for transfers between devices  47.5 us (12%)
  matrix products  17.9 us (4%)
  between operations  4.08 us (1%)
    psum x10, blocking collectives, one_axis_at_a_time(): array = lax.psum(array, axis)  104 us
    concatenate x6, other arithmetic, extended(): block = jnp.concatenate([low, block, high], axis=dim)  36.1 us
    slice x10, local copies, waits for them, and re-layouts, extended(): lax.slice_in_dim(block, block.shape[dim] - width, None, axis=dim)  35.3 us
    ppermute x10, starting transfers between devices, extended(): lax.ppermute(lax.slice_in_dim(block, block.shape[dim] - width, None, axis...  33.7 us
    ppermute x10, waiting for transfers between devices, extended(): lax.ppermute(lax.slice_in_dim(block, block.shape[dim] - width, None, axis...  33.5 us
    ppermute x10, starting transfers between devices, extended(): lax.ppermute(lax.slice_in_dim(block, 0, width, axis=dim), axis, backward)  24 us
    select_n x3, other arithmetic, advance_deep(): jnp.where(valid_rows[None, :, None], wide_height, jnp.zeros_like(wide_hei...  17.3 us
    slice x5, local copies, waits for them, and re-layouts, extended(): lax.slice_in_dim(block, 0, width, axis=dim)  17.1 us
  transfers between devices with their start and end apart: 20, of which 10 were waited for; matrix products, arithmetic and copies ran while one was open for 9% of the time, Pallas kernels for 0%

commit v1 on v0

v1 whole, which is shorter than its diff:
```python
import functools
import math

import jax
import jax.numpy as jnp
from jax import lax
from jax.experimental import pallas as pl
from jax.experimental.pallas import tpu as pltpu
from jax.sharding import PartitionSpec as P

MESH = pl.DeviceIdType.MESH
F32 = jnp.float32
BF16 = jnp.bfloat16

MEMBERS = 80
ROWS = 32
COLS = 128
NMEM = 16
NBAND = 8
STEPS = 3
LSCALE = 12.0
REACH = 32
GROUPS = 11
MEAN = 80
CHUNK = 16
NCHUNK = MEMBERS // CHUNK
QUADS = CHUNK // 4
CELLS = float(MEMBERS * 512 * 1024)


def taper(offset):
    scaled = offset.astype(F32) / LSCALE
    weight = jnp.exp(-0.5 * scaled * scaled)
    return jnp.where(jnp.abs(offset) <= REACH, weight, 0.0)


def split(x):
    high = x.astype(BF16)
    low = (x - high.astype(F32)).astype(BF16)
    return high, low


def build_tapers(lat_k, lon_k):
    i = lax.broadcasted_iota(jnp.int32, (64, 192), 0)
    j = lax.broadcasted_iota(jnp.int32, (64, 192), 1)
    a = jnp.where(i < 32, i, i - 32)
    jj = jnp.where(j < 96, j, j - 96)
    w = taper(jj - 32 - a)
    high = w.astype(BF16).astype(F32)
    low = jnp.where(j < 96, w - high, 0.0)
    lat_k[...] = jnp.where(i < 32, high, low).astype(BF16)
    for s in range(4):
        for block in range(3):
            k = lax.broadcasted_iota(jnp.int32, (128, 256), 0)
            n = lax.broadcasted_iota(jnp.int32, (128, 256), 1)
            out = jnp.where(n < 128, n, n - 128)
            if block == 0:
                w = taper(k - out)
            else:
                inside = (k >= 32 * s) & (k < 32 * s + 32)
                start = -32 if block == 1 else 128
                w = jnp.where(inside, taper(k - 32 * s + start - out), 0.0)
            high = w.astype(BF16).astype(F32)
            lon_k[s, pl.ds(128 * block, 128), :] = jnp.where(n < 128, high, w - high).astype(BF16)


def kernel(
    h_in, u_in, v_in, obs_value, obs_mask, obs_precision, steps,
    h_out, u_out, v_out, inc,
    x, f, rh, ps, pr, c, rc, lt, ls, lr, g1, lat_k, lon_k, coef, state, s_acc, sq, red,
    load_sem, store_sem, halo_ss, halo_rs, row_ss, row_rs, col_ss, col_rs, red_ss, red_rs,
):
    m = lax.axis_index("member")
    b = lax.axis_index("band")
    has_up = m > 0
    has_dn = m < NMEM - 1
    up = lax.rem(m + NMEM - 1, NMEM)
    dn = lax.rem(m + 1, NMEM)
    lf = lax.rem(b + NBAND - 1, NBAND)
    rt = lax.rem(b + 1, NBAND)

    core = lax.rem(m, 2)
    y = lax.rem(m // 2, 4)
    z_lo = m // 8
    xx = b // 2
    z = lax.rem(b, 2) * 2 + z_lo

    def at(core_, y_, x_, z_):
        return ((lax.rem(z_, 2) * 4 + y_) * 2 + core_, x_ * 2 + z_ // 2)

    stages = [
        [at(1 - core, y, xx, z)],
        [at(core, lax.rem(y + j, 4), xx, z) for j in (1, 2, 3)],
        [at(core, y, lax.rem(xx + j, 4), z) for j in (1, 2, 3)],
        [at(core, y, xx, lax.rem(z + j, 4)) for j in (1, 2, 3)],
    ]

    near = [(up, b), (dn, b), (m, lf), (m, rt), (up, lf), (up, rt), (dn, lf), (dn, rt)]
    greet = near + [d for stage in stages for d in stage]
    barrier = pltpu.get_barrier_semaphore()
    for d in greet:
        pl.semaphore_signal(barrier, inc=1, device_id=d, device_id_type=MESH)

    loads = [
        pltpu.make_async_copy(src, x.at[k, pl.ds(0, MEMBERS)], load_sem.at[k])
        for k, src in enumerate((h_in, u_in, v_in))
    ]
    for copy in loads:
        copy.start()

    @pl.when(m == 0)
    def _():
        rh[:, 0] = jnp.zeros((3, 8 * GROUPS, 8, COLS), F32)
        pr[:, :, pl.ds(0, 8), :] = jnp.zeros((2, GROUPS, 8, COLS), F32)
        rc[0, 0] = jnp.zeros((MEMBERS, ROWS, COLS), F32)
        rc[1, 0] = jnp.zeros((MEMBERS, ROWS, COLS), F32)

    @pl.when(m == NMEM - 1)
    def _():
        rh[:, 1] = jnp.zeros((3, 8 * GROUPS, 8, COLS), F32)
        pr[:, :, pl.ds(40, 8), :] = jnp.zeros((2, GROUPS, 8, COLS), F32)
        rc[0, 1] = jnp.zeros((MEMBERS, ROWS, COLS), F32)
        rc[1, 1] = jnp.zeros((MEMBERS, ROWS, COLS), F32)

    build_tapers(lat_k, lon_k)
    x[:, pl.ds(MEAN + 1, 7)] = jnp.zeros((3, 7, ROWS, COLS), F32)

    for copy in loads:
        copy.wait()

    for k in range(3):
        x[k, MEAN] = lax.fori_loop(
            0, MEMBERS, lambda i, total, k=k: total + x[k, i], jnp.zeros((ROWS, COLS), F32), unroll=8
        ) * (1.0 / MEMBERS)

    lane = lax.broadcasted_iota(jnp.int32, (ROWS, COLS), 1)

    def pack(g):
        left = jnp.zeros((ROWS, COLS), F32)
        right = jnp.zeros((ROWS, COLS), F32)
        for s in range(8):
            base = 16 * s
            i = g * 8 + s
            for field, lo, width in ((1, 0, 6), (0, 6, 5), (2, 11, 5)):
                value = x[field, i]
                where = (lane >= base + lo) & (lane < base + lo + width)
                left = jnp.where(where, pltpu.roll(value, base + lo, 1), left)
                right = jnp.where(where, pltpu.roll(value, (base + lo + width) % COLS, 1), right)
        ps[0, g] = left
        ps[1, g] = right

    def halo_copy(k, g):
        members = pl.ds(g * 8, 8)
        top, bottom, body = pl.ds(0, 8), pl.ds(24, 8), pl.ds(8, 32)
        below = pl.ds(40, 8)
        src, dst = (
            (x.at[:, members, top], rh.at[:, 1, members]),
            (x.at[:, members, bottom], rh.at[:, 0, members]),
            (ps.at[0, g], pr.at[1, g, body]),
            (ps.at[1, g], pr.at[0, g, body]),
            (ps.at[0, g, top], pr.at[1, g, below]),
            (ps.at[1, g, top], pr.at[0, g, below]),
            (ps.at[0, g, bottom], pr.at[1, g, top]),
            (ps.at[1, g, bottom], pr.at[0, g, top]),
        )[k]
        return pltpu.make_async_remote_copy(
            src_ref=src, dst_ref=dst, send_sem=halo_ss.at[g, k], recv_sem=halo_rs.at[g, k],
            device_id=near[k], device_id_type=MESH,
        )

    def halo_start(g):
        @pl.when(has_up)
        def _():
            for k in (0, 4, 5):
                halo_copy(k, g).start()

        @pl.when(has_dn)
        def _():
            for k in (1, 6, 7):
                halo_copy(k, g).start()

        for k in (2, 3):
            halo_copy(k, g).start()

    def halo_wait(g):
        @pl.when(has_up)
        def _():
            for k in (1, 6, 7):
                halo_copy(k, g).wait_recv()
            for k in (0, 4, 5):
                halo_copy(k, g).wait_send()

        @pl.when(has_dn)
        def _():
            for k in (0, 4, 5):
                halo_copy(k, g).wait_recv()
            for k in (1, 6, 7):
                halo_copy(k, g).wait_send()

        for k in (2, 3):
            halo_copy(k, g).wait_recv()
            halo_copy(k, g).wait_send()

    pack(MEAN // 8)
    pl.semaphore_wait(barrier, len(greet))
    halo_start(MEAN // 8)

    def send_halo(g, carry):
        pack(g)
        halo_start(g)
        return carry

    lax.fori_loop(0, MEMBERS // 8, send_halo, 0)

    elane = lax.broadcasted_iota(jnp.int32, (48, COLS), 1)
    first, last, half = elane == 0, elane == COLS - 1, elane < 64
    erow = lax.broadcasted_iota(jnp.int32, (48, COLS), 0)
    inside = ((erow >= 8) | has_up) & ((erow < 40) | has_dn)

    def lon_diff(pair):
        main, side = pair
        em, es = pltpu.roll(main, COLS - 1, 1), pltpu.roll(side, COLS - 1, 1)
        wm, ws = pltpu.roll(main, 1, 1), pltpu.roll(side, 1, 1)
        return (
            jnp.where(last, es, em) - jnp.where(first, ws, wm),
            jnp.where(last, em, es) - jnp.where(first, wm, ws),
        )

    def lat_diff(pair):
        return tuple(pltpu.roll(q, 47, 0) - pltpu.roll(q, 1, 0) for q in pair)

    def forecast(g, s):
        i = g * 8 + s
        from_left, from_right = pr[0, g], pr[1, g]
        fields = []
        for k, lo, width in ((0, 6, 5), (1, 0, 6), (2, 11, 5)):
            main = jnp.concatenate([rh[k, 0, i], x[k, i], rh[k, 1, i]], axis=0)
            right = pltpu.roll(from_right, lax.rem(2 * COLS - lo - 16 * s, COLS), 1)
            left = pltpu.roll(from_left, lax.rem(2 * COLS - width - lo - 16 * s, COLS), 1)
            fields.append((main, jnp.where(half, right, left)))
        hh, uu, vv = fields
        for _ in range(STEPS):
            du, dv = lon_diff(uu), lat_diff(vv)
            hn = tuple(jnp.where(inside, hh[p] - 0.2 * (du[p] + dv[p]), 0.0) for p in range(2))
            dx, dy = lon_diff(hn), lat_diff(hn)
            un = tuple(uu[p] + 0.1 * vv[p] - 0.2 * dx[p] for p in range(2))
            vn = tuple(jnp.where(inside, vv[p] - 0.1 * uu[p] - 0.2 * dy[p], 0.0) for p in range(2))
            hh, uu, vv = hn, un, vn
        return hh[0][8:40], uu[0][8:40], vv[0][8:40]

    halo_wait(MEAN // 8)
    mean = forecast(MEAN // 8, 0)
    for k in range(3):
        state[k] = mean[k]
    obs_weight = obs_mask[...].astype(F32) * obs_precision[...]

    def set_coefficients(sh, su, sv):
        residual = obs_weight * (obs_value[...] - sh - 0.15 * (su * su + sv * sv))
        coef[0] = residual
        coef[1] = 0.3 * su * residual
        coef[2] = 0.3 * sv * residual

    set_coefficients(*mean)

    def row_copy(it, k, n):
        members = pl.ds(n * CHUNK, CHUNK)
        return pltpu.make_async_remote_copy(
            src_ref=c.at[members], dst_ref=rc.at[it, 1 - k, members],
            send_sem=row_ss.at[it, k, n], recv_sem=row_rs.at[it, k, n],
            device_id=near[k], device_id_type=MESH,
        )

    def row_start(it, n):
        @pl.when(has_up)
        def _():
            row_copy(it, 0, n).start()

        @pl.when(has_dn)
        def _():
            row_copy(it, 1, n).start()

    def row_wait(it, n):
        @pl.when(has_up)
        def _():
            row_copy(it, 1, n).wait_recv()

        @pl.when(has_dn)
        def _():
            row_copy(it, 0, n).wait_recv()

    def row_sent(it, n):
        @pl.when(has_up)
        def _():
            row_copy(it, 0, n).wait_send()

        @pl.when(has_dn)
        def _():
            row_copy(it, 1, n).wait_send()

    def col_copy(it, k, n):
        quads = pl.ds(n * QUADS, QUADS)
        return pltpu.make_async_remote_copy(
            src_ref=ls.at[k, quads], dst_ref=lr.at[it, 1 - k, quads],
            send_sem=col_ss.at[it, k, n], recv_sem=col_rs.at[it, k, n],
            device_id=near[2 + k], device_id_type=MESH,
        )

    scale = 1.0 / math.sqrt(MEMBERS - 1.0)

    def first_chunk(n, carry):
        for gg in range(CHUNK // 8):
            g = n * (CHUNK // 8) + gg
            halo_wait(g)

            def one(s, carry2, g=g):
                i = g * 8 + s
                out = forecast(g, s)
                total = None
                for k in range(3):
                    f[k, i] = out[k]
                    anomaly = (out[k] - state[k]) * scale
                    x[k, i] = anomaly
                    term = anomaly * coef[k]
                    total = term if total is None else total + term
                c[i] = total
                return carry2

            lax.fori_loop(0, 8, one, 0)
        row_start(0, n)
        return carry

    lax.fori_loop(0, NCHUNK, first_chunk, 0)

    stores = [
        pltpu.make_async_copy(f.at[k], dst, store_sem.at[k])
        for k, dst in enumerate((h_out, u_out, v_out))
    ]
    for copy in stores:
        copy.start()

    def taper_rows(it, n):
        row_wait(it, n)

        def quad(q, carry):
            parts_high, parts_low = [], []
            for ref_part in range(3):
                wide = []
                for s in range(4):
                    i = q * 4 + s
                    wide.append(rc[it, 0, i] if ref_part == 0 else (c[i] if ref_part == 1 else rc[it, 1, i]))
                high, low = split(jnp.concatenate(wide, axis=1))
                parts_high.append(high)
                parts_low.append(low)
            right_side = jnp.concatenate(parts_high + parts_low, axis=0)
            both = jnp.dot(lat_k[...], right_side, preferred_element_type=F32)
            lat = both[:32] + both[32:]
            to_left = jnp.zeros((ROWS, COLS), F32)
            to_right = jnp.zeros((ROWS, COLS), F32)
            for s in range(4):
                part = lat[:, s * COLS:(s + 1) * COLS]
                lt[s, q] = part
                where = (lane >= 32 * s) & (lane < 32 * s + 32)
                to_left = jnp.where(where, pltpu.roll(part, 32 * s, 1) if s else part, to_left)
                to_right = jnp.where(where, pltpu.roll(part, 32 * s + 32, 1) if s < 3 else part, to_right)
            ls[0, q] = to_left
            ls[1, q] = to_right
            return carry

        lax.fori_loop(n * QUADS, (n + 1) * QUADS, quad, 0)
        for k in range(2):
            col_copy(it, k, n).start()

    def taper_cols(it, n, factor):
        for k in range(2):
            col_copy(it, k, n).wait_recv()
        quads = pl.ds(n * QUADS, QUADS)
        size = QUADS * ROWS
        lh, ll = split(lr[it, 0, quads].reshape(size, COLS))
        rhh, rl = split(lr[it, 1, quads].reshape(size, COLS))
        totals = [None] * 4
        for s in range(4):
            mh, ml = split(lt[s, quads].reshape(size, COLS))
            a = jnp.dot(jnp.concatenate([mh, lh, rhh], axis=1), lon_k[s], preferred_element_type=F32)
            d = jnp.dot(jnp.concatenate([ml, ll, rl], axis=1), lon_k[s, :, pl.ds(0, 128)], preferred_element_type=F32)
            g = (a[:, :COLS] + a[:, COLS:] + d).reshape(QUADS, ROWS, COLS)
            if it == 0:
                g1[s, quads] = g
            else:
                g = factor * g1[s, quads] - g
            for qq in range(QUADS):
                i = (n * QUADS + qq) * 4 + s
                part = g[qq]
                terms = [x[k, i] * part for k in range(3)] + [part * part]
                totals = [t if o is None else o + t for o, t in zip(totals, terms)]
        for k in range(3):
            s_acc[it, k] += totals[k]
        sq[...] += totals[3]

    def localize(it, factor):
        def body(n, carry):
            @pl.when(n < NCHUNK)
            def _():
                taper_rows(it, n)

            @pl.when(n > 0)
            def _():
                taper_cols(it, n - 1, factor)

            return carry

        lax.fori_loop(0, NCHUNK + 1, body, 0)

    def sum_all(it):
        value = sq[...]
        value = value[:8] + value[8:16] + value[16:24] + value[24:]
        slot = 0
        for stage in stages:
            red[it, slot] = value
            copies = [
                pltpu.make_async_remote_copy(
                    src_ref=red.at[it, slot], dst_ref=red.at[it, slot + 1 + j],
                    send_sem=red_ss.at[it, slot + j], recv_sem=red_rs.at[it, slot + j],
                    device_id=d, device_id_type=MESH,
                )
                for j, d in enumerate(stage)
            ]
            for copy in copies:
                copy.start()
            for copy in copies:
                copy.wait_recv()
            for j in range(len(stage)):
                value = value + red[it, slot + 1 + j]
            for copy in copies:
                copy.wait_send()
            slot += 1 + len(stage)
        total = jnp.sum(jnp.sum(value, axis=0, keepdims=True), axis=1, keepdims=True)
        return steps[it].astype(F32) / 64.0 / jnp.sqrt(total / CELLS + 1e-6)

    for it in range(2):
        for k in range(3):
            s_acc[it, k] = jnp.zeros((ROWS, COLS), F32)
    sq[...] = jnp.zeros((ROWS, COLS), F32)
    localize(0, None)
    factor1 = sum_all(0)

    def sent(n, carry):
        row_sent(0, n)
        for k in range(2):
            col_copy(0, k, n).wait_send()
        return carry

    lax.fori_loop(0, NCHUNK, sent, 0)
    sq[...] = jnp.zeros((ROWS, COLS), F32)
    set_coefficients(*[state[k] + factor1 * s_acc[0, k] for k in range(3)])

    def second_chunk(n, carry):
        def one(j, carry2):
            i = n * CHUNK + j
            c[i] = x[0, i] * coef[0] + x[1, i] * coef[1] + x[2, i] * coef[2]
            return carry2

        lax.fori_loop(0, CHUNK, one, 0, unroll=4)
        row_start(1, n)
        return carry

    lax.fori_loop(0, NCHUNK, second_chunk, 0)
    localize(1, factor1)
    factor2 = sum_all(1)
    for k in range(3):
        inc[k] = factor1 * s_acc[0, k] - factor2 * s_acc[1, k]

    def sent2(n, carry):
        row_sent(1, n)
        for k in range(2):
            col_copy(1, k, n).wait_send()
        return carry

    lax.fori_loop(0, NCHUNK, sent2, 0)
    for copy in stores:
        copy.wait()


def per_device(height, east, north, obs_value, obs_mask, obs_precision, step_sizes):
    block = (MEMBERS, ROWS, COLS)
    vmem = pl.BlockSpec(memory_space=pltpu.VMEM)
    anyspace = pl.BlockSpec(memory_space=pl.ANY)
    dma = pltpu.SemaphoreType.DMA
    h, u, v, inc = pl.pallas_call(
        kernel,
        name="analysis",
        out_shape=[jax.ShapeDtypeStruct(block, F32)] * 3 + [jax.ShapeDtypeStruct((3, ROWS, COLS), F32)],
        in_specs=[anyspace] * 3 + [vmem] * 3 + [pl.BlockSpec(memory_space=pltpu.SMEM)],
        out_specs=[anyspace] * 3 + [vmem],
        scratch_shapes=[
            pltpu.VMEM((3, 8 * GROUPS, ROWS, COLS), F32),
            pltpu.VMEM((3, MEMBERS, ROWS, COLS), F32),
            pltpu.VMEM((3, 2, 8 * GROUPS, 8, COLS), F32),
            pltpu.VMEM((2, GROUPS, ROWS, COLS), F32),
            pltpu.VMEM((2, GROUPS, 48, COLS), F32),
            pltpu.VMEM(block, F32),
            pltpu.VMEM((2, 2) + block, F32),
            pltpu.VMEM((4, MEMBERS // 4, ROWS, COLS), F32),
            pltpu.VMEM((2, MEMBERS // 4, ROWS, COLS), F32),
            pltpu.VMEM((2, 2, MEMBERS // 4, ROWS, COLS), F32),
            pltpu.VMEM((4, MEMBERS // 4, ROWS, COLS), F32),
            pltpu.VMEM((64, 192), BF16),
            pltpu.VMEM((4, 384, 256), BF16),
            pltpu.VMEM((3, ROWS, COLS), F32),
            pltpu.VMEM((3, ROWS, COLS), F32),
            pltpu.VMEM((2, 3, ROWS, COLS), F32),
            pltpu.VMEM((ROWS, COLS), F32),
            pltpu.VMEM((2, 14, 8, COLS), F32),
            dma((3,)), dma((3,)),
            dma((GROUPS, 8)), dma((GROUPS, 8)),
            dma((2, 2, NCHUNK)), dma((2, 2, NCHUNK)),
            dma((2, 2, NCHUNK)), dma((2, 2, NCHUNK)),
            dma((2, 14)), dma((2, 14)),
        ],
        compiler_params=pltpu.CompilerParams(
            collective_id=0, has_side_effects=True, vmem_limit_bytes=48 << 20
        ),
    )(height, east, north, obs_value, obs_mask, obs_precision, step_sizes)
    return h + inc[0], u + inc[1], v + inc[2]


def solution(mesh):
    spec3 = P(None, "member", "band")
    spec2 = P("member", "band")
    return jax.shard_map(
        per_device,
        mesh=mesh,
        in_specs=(spec3, spec3, spec3, spec2, spec2, spec2, P()),
        out_specs=(spec3, spec3, spec3),
        check_vma=False,
    )
```

time: 406 us -> 170 us (0.42); the launches traced: 401 us -> 170 us
  Pallas kernels: 0 us -> 162 us
  blocking collectives: 104 us -> 0 us
  local copies, waits for them, and re-layouts: 101 us -> 4.12 us
  other arithmetic: 68.6 us -> 2.97 us
  starting transfers between devices: 57.7 us -> 0 us
  waiting for transfers between devices: 47.5 us -> 0 us
  matrix products: 17.9 us -> 0 us
    pallas_call x0 -> x1, Pallas kernels: none -> 162 us  [per_device(): pl.pallas_call(kernel, name='analysis', out_shape=[jax.ShapeDtypeStruct(b...]
    psum x10 -> x0, blocking collectives: 104 us -> none  [one_axis_at_a_time(): array = lax.psum(array, axis)]
    ppermute x20 -> x0, starting transfers between devices: 57.7 us -> none  [the longest x10 33.7 us: extended(): lax.ppermute(lax.slice_in_dim(block, block.shape[dim] - width, None, axis...]
    slice x16 -> x0, local copies, waits for them, and re-layouts: 53 us -> none  [the longest x10 35.3 us: extended(): lax.slice_in_dim(block, block.shape[dim] - width, None, axis=dim)]
    ppermute x20 -> x0, waiting for transfers between devices: 47.5 us -> none  [the longest x10 33.5 us: extended(): lax.ppermute(lax.slice_in_dim(block, block.shape[dim] - width, None, axis...]
    concatenate x6 -> x0, other arithmetic: 36.1 us -> none  [extended(): block = jnp.concatenate([low, block, high], axis=dim)]
    ppermute x10 -> x0, local copies, waits for them, and re-layouts: 33.4 us -> none  [the longest x5 16.8 us: extended(): lax.ppermute(lax.slice_in_dim(block, block.shape[dim] - width, None, axis...]
    dot_general x4 -> x0, matrix products: 17.9 us -> none  [the longest x2 13.2 us: taper_columns(): result = jnp.einsum('mrjk,bk->mrjb', windows, kernel, precision=highest)]
  transfers between devices with their start and end apart: 20 -> 0, of which waited for: 10 -> 0; matrix products, arithmetic and copies ran while one was open for 9% -> 0% of each run, Pallas kernels for 0% -> 0%
where the time goes in v1:
time: 170 us
  Pallas kernels  162 us (95%)
  local copies, waits for them, and re-layouts  4.12 us (2%)
  other arithmetic  2.97 us (2%)
    pallas_call x1, Pallas kernels, per_device(): pl.pallas_call(kernel, name='analysis', out_shape=[jax.ShapeDtypeStruct(b...  162 us
    unnamed x10, local copies, waits for them, and re-layouts  4.11 us

profile of v1, /device:TPU:0, one launch (start us, length us, event | category | flops | bytes accessed | tf_op | source)
XLA Modules:
  0.0 170.0 jit_solution(16164750371034670947)
XLA Ops:
  0.6 0.0 copy-start
  0.6 1.3 copy-done
  1.9 0.0 copy-start.1
  2.0 0.7 copy-done.1
  2.7 0.0 copy-start.2
  2.7 0.7 copy-done.2
  3.4 0.0 copy-start.3
  3.4 0.7 copy-done.3
  4.1 0.0 copy-start.4
  4.1 0.7 copy-done.4
  4.8 162.3 %analysis.1 = (f32[80,32,128]{2,1,0:T(8,128)S(1)}, f32[80,32,128]{2,1,0:T(8,128)S(1)}, f32[80,32,128]{2,1,0:T(8,128)S(1)}, f32[3,32,128]{2,1,0:T(8,128)S(1)}) custom-call(f32[80,32,128]{2,1,0:T(8,128)S(1)} %copy-done, f32[80,32,128]{2,1,0:T(8,128)} %u_in.1, f32[80,32,128]{2,1,0:T(8,128)} %v_in.1, f32[32,128]{1,0:T(8,128)S(1)} %copy-done.1, ...), custom_call_target="tpu_custom_call" | custom-call | tf_op jit(solution)/shard_map/analysis/pallas_call | solution.py:488
  167.1 1.2 broadcast_add_fusion.2
  168.2 1.8 %broadcast_add_fusion = (f32[80,32,128]{2,1,0:T(8,128)}, f32[80,32,128]{2,1,0:T(8,128)}) fusion(f32[80,32,128]{2,1,0:T(8,128)S(1)} %get-tuple-element.10, f32[32,128]{1,0:T(8,128)S(1)} %get-tuple-element.11, f32[80,32,128]{2,1,0:T(8,128)S(1)} %get-tuple-element.9, f32[32,128]{1,0:T(8,128)S(1)} %get-tuple-element.12), kind=kLoop, calls=%fused_computation | loop fusion | flops 655360 | bytes 5275648 | tf_op jit(solution)/shard_map/add | solution.py:523
  (1 shorter events, 0.0 us)
Async XLA Ops:
  0.6 1.3 copy-start
  1.9 0.7 copy-start.1
  2.7 0.7 copy-start.2
  3.4 0.7 copy-start.3
  4.1 0.7 copy-start.4

commit v2 on v1

v2 whole, which is shorter than its diff:
```python
import functools
import math

import jax
import jax.numpy as jnp
from jax import lax
from jax.experimental import pallas as pl
from jax.experimental.pallas import tpu as pltpu
from jax.sharding import PartitionSpec as P

MESH = pl.DeviceIdType.MESH
F32 = jnp.float32
BF16 = jnp.bfloat16

MEMBERS = 80
ROWS = 32
COLS = 128
NMEM = 16
NBAND = 8
STEPS = 3
LSCALE = 12.0
REACH = 32
GROUPS = 11
MEAN = 80
CHUNK = 8
NCHUNK = MEMBERS // CHUNK
QUADS = CHUNK // 4
NHALO = MEMBERS // 16
SKEW = 5
TOGETHER = 8
ABOVE, OWN, BELOW = pl.ds(0, 8), pl.ds(8, 32), pl.ds(40, 8)
TOP, BOTTOM = pl.ds(8, 8), pl.ds(32, 8)
CELLS = float(MEMBERS * 512 * 1024)


def taper(offset):
    scaled = offset.astype(F32) / LSCALE
    weight = jnp.exp(-0.5 * scaled * scaled)
    return jnp.where(jnp.abs(offset) <= REACH, weight, 0.0)


def split(x):
    high = x.astype(BF16)
    low = (x - high.astype(F32)).astype(BF16)
    return high, low


def build_tapers(lat_k, lon_k):
    i = lax.broadcasted_iota(jnp.int32, (64, 192), 0)
    j = lax.broadcasted_iota(jnp.int32, (64, 192), 1)
    a = jnp.where(i < 32, i, i - 32)
    jj = jnp.where(j < 96, j, j - 96)
    w = taper(jj - 32 - a)
    high = w.astype(BF16).astype(F32)
    low = jnp.where(j < 96, w - high, 0.0)
    lat_k[...] = jnp.where(i < 32, high, low).astype(BF16)
    k = lax.broadcasted_iota(jnp.int32, (COLS, 2 * COLS), 0)
    n = lax.broadcasted_iota(jnp.int32, (COLS, 2 * COLS), 1)

    def lon(w, n):
        high = w.astype(BF16).astype(F32)
        return jnp.where(n < COLS, high, w - high).astype(BF16)

    out = jnp.where(n < COLS, n, n - COLS)
    own = lon(taper(k - out), n)
    k, n, out = k[:32], n[:32], out[:32]
    left, right = lon(taper(k - 32 - out), n), lon(taper(k + COLS - out), n)
    for s in range(4):
        lon_k[s, pl.ds(0, COLS), :] = own
        lon_k[s, pl.ds(COLS, 2 * COLS), :] = jnp.zeros((2 * COLS, 2 * COLS), BF16)
        lon_k[s, pl.ds(COLS + 32 * s, 32), :] = left
        lon_k[s, pl.ds(2 * COLS + 32 * s, 32), :] = right


def kernel(
    h_in, u_in, v_in, value_in, mask_in, precision_in, steps_in,
    h_out, u_out, v_out, inc,
    x, f, ps, pr, c, rc, lt, ls, lr, g1, lat_k, lon_k, coef, state, s_acc, sq, red,
    obs_value, obs_mask, obs_precision, steps, strip, relay,
    load_sem, store_sem, halo_ss, halo_rs, row_ss, row_rs, relay_rs, col_ss, col_rs, red_ss, red_rs,
):
    m = lax.axis_index("member")
    b = lax.axis_index("band")
    has_up = m > 0
    has_dn = m < NMEM - 1
    up = lax.rem(m + NMEM - 1, NMEM)
    dn = lax.rem(m + 1, NMEM)
    lf = lax.rem(b + NBAND - 1, NBAND)
    rt = lax.rem(b + 1, NBAND)

    core = lax.rem(m, 2)
    y = lax.rem(m // 2, 4)
    z_lo = m // 8
    xx = b // 2
    z = lax.rem(b, 2) * 2 + z_lo

    def at(core_, y_, x_, z_):
        return ((lax.rem(z_, 2) * 4 + y_) * 2 + core_, x_ * 2 + z_ // 2)

    stages = [
        [at(1 - core, y, xx, z)],
        [at(core, lax.rem(y + j, 4), xx, z) for j in (1, 2, 3)],
        [at(core, y, lax.rem(xx + j, 4), z) for j in (1, 2, 3)],
        [at(core, y, xx, lax.rem(z + j, 4)) for j in (1, 2, 3)],
    ]

    near = [(up, b), (dn, b), (m, lf), (m, rt), (up, lf), (up, rt), (dn, lf), (dn, rt)]
    mirror = (z_lo * 8 + 7 - lax.rem(m, 8), b)
    greet = near + [mirror] + [d for stage in stages for d in stage]
    barrier = pltpu.get_barrier_semaphore()
    for d in greet:
        pl.semaphore_signal(barrier, inc=1, device_id=d, device_id_type=MESH)

    loads = [
        pltpu.make_async_copy(src, dst, load_sem.at[k])
        for k, (src, dst) in enumerate((
            (h_in, x.at[0, pl.ds(0, MEMBERS), OWN]),
            (u_in, x.at[1, pl.ds(0, MEMBERS), OWN]),
            (v_in, x.at[2, pl.ds(0, MEMBERS), OWN]),
            (value_in, obs_value),
            (mask_in, obs_mask),
            (precision_in, obs_precision),
            (steps_in, steps),
        ))
    ]
    for copy in loads:
        copy.start()

    lane = lax.broadcasted_iota(jnp.int32, (ROWS, COLS), 1)

    def pack(g, count):
        left = jnp.zeros((ROWS, COLS), F32)
        right = jnp.zeros((ROWS, COLS), F32)
        for s in range(count):
            base = 16 * s
            i = g * 8 + s
            for field, lo, width in ((1, 0, 6), (0, 6, 5), (2, 11, 5)):
                value = x[field, i, OWN]
                where = (lane >= base + lo) & (lane < base + lo + width)
                left = jnp.where(where, pltpu.roll(value, base + lo, 1), left)
                right = jnp.where(where, pltpu.roll(value, (base + lo + width) % COLS, 1), right)
        ps[0, g, OWN] = left
        ps[1, g, OWN] = right

    def halo_copy(k, n, mean=False):
        members = pl.ds(MEAN, 1) if mean else pl.ds(n * 16, 16)
        groups = pl.ds(MEAN // 8, 1) if mean else pl.ds(n * 2, 2)
        src, dst, to = (
            (x.at[:, members, TOP], x.at[:, members, BELOW], (up, b)),
            (ps.at[:, groups, TOP], ps.at[:, groups, BELOW], (up, b)),
            (ps.at[0, groups, TOP], pr.at[1, groups, BELOW], (up, lf)),
            (ps.at[1, groups, TOP], pr.at[0, groups, BELOW], (up, rt)),
            (x.at[:, members, BOTTOM], x.at[:, members, ABOVE], (dn, b)),
            (ps.at[:, groups, BOTTOM], ps.at[:, groups, ABOVE], (dn, b)),
            (ps.at[0, groups, BOTTOM], pr.at[1, groups, ABOVE], (dn, lf)),
            (ps.at[1, groups, BOTTOM], pr.at[0, groups, ABOVE], (dn, rt)),
            (ps.at[0, groups, OWN], pr.at[1, groups, OWN], (m, lf)),
            (ps.at[1, groups, OWN], pr.at[0, groups, OWN], (m, rt)),
        )[k]
        return pltpu.make_async_remote_copy(
            src_ref=src, dst_ref=dst, send_sem=halo_ss.at[n, k], recv_sem=halo_rs.at[n, k],
            device_id=to, device_id_type=MESH,
        )

    def halo_start(n, mean=False):
        for k in (8, 9):
            halo_copy(k, n, mean).start()

        @pl.when(has_up)
        def _():
            for k in range(0, 4):
                halo_copy(k, n, mean).start()

        @pl.when(has_dn)
        def _():
            for k in range(4, 8):
                halo_copy(k, n, mean).start()

    def halo_wait(n, mean=False):
        @pl.when(has_up)
        def _():
            for k in range(4, 8):
                halo_copy(k, n, mean).wait_recv()
            for k in range(0, 4):
                halo_copy(k, n, mean).wait_send()

        @pl.when(has_dn)
        def _():
            for k in range(0, 4):
                halo_copy(k, n, mean).wait_recv()
            for k in range(4, 8):
                halo_copy(k, n, mean).wait_send()

        for k in (8, 9):
            halo_copy(k, n, mean).wait_recv()
            halo_copy(k, n, mean).wait_send()

    def send_halo(n, carry):
        for gg in range(2):
            pack(2 * n + gg, 8)
        halo_start(n)
        return carry

    for copy in loads:
        copy.wait()
    for gg in range(2):
        pack(gg, 8)
    pl.semaphore_wait(barrier, len(greet))
    halo_start(0)

    for k in range(3):
        x[k, MEAN, OWN] = lax.fori_loop(
            0, MEMBERS, lambda i, total, k=k: total + x[k, i, OWN], jnp.zeros((ROWS, COLS), F32), unroll=8
        ) * (1.0 / MEMBERS)
    pack(MEAN // 8, 1)
    halo_start(NHALO, True)

    lax.fori_loop(1, NHALO, send_halo, 0)

    def clear(halo, side):
        x[:, :, halo, :] = jnp.zeros((3, MEMBERS + 8, 8, COLS), F32)
        ps[:, :, halo, :] = jnp.zeros((2, GROUPS, 8, COLS), F32)
        pr[:, :, halo, :] = jnp.zeros((2, GROUPS, 8, COLS), F32)
        for it in range(2):
            rc[it, side] = jnp.zeros((MEMBERS, ROWS, COLS), F32)

    @pl.when(m == 0)
    def _():
        clear(ABOVE, 0)

    @pl.when(m == NMEM - 1)
    def _():
        clear(BELOW, 1)

    build_tapers(lat_k, lon_k)

    tile = lax.broadcasted_iota(jnp.int32, (8, COLS), 0)
    column = lax.broadcasted_iota(jnp.int32, (8, COLS), 1)
    inside = [
        ((6 * tile + j >= 8) | has_up) & ((6 * tile + j < 40) | has_dn) for j in range(6)
    ]
    place = lax.rem(column, 16)
    edge = (column < 6) | (column >= COLS - 6)

    def lon_diff(q):
        return [pltpu.roll(w, COLS - 1, 1) - pltpu.roll(w, 1, 1) for w in q]

    def lat_diff(q):
        out = []
        for first in range(0, len(q), 6):
            part = q[first:first + 6]
            after = part[1:] + [pltpu.roll(part[0], 7, 0)]
            before = [pltpu.roll(part[5], 1, 0)] + part[:5]
            out += [p - w for p, w in zip(after, before)]
        return out

    def advance(hh, uu, vv, keep):
        six = range(len(hh))
        for _ in range(STEPS):
            du, dv = lon_diff(uu), lat_diff(vv)
            hn = [jnp.where(keep[j % 6], hh[j] - 0.2 * (du[j] + dv[j]), 0.0) for j in six]
            dx, dy = lon_diff(hn), lat_diff(hn)
            un = [uu[j] + 0.1 * vv[j] - 0.2 * dx[j] for j in six]
            vn = [jnp.where(inside[j % 6], vv[j] - 0.1 * uu[j] - 0.2 * dy[j], 0.0) for j in six]
            hh, uu, vv = hn, un, vn
        return hh, uu, vv

    def strided(j):
        return pl.ds(j, 8, stride=6)

    def strips(g):
        keep = [w & (place < 12) for w in inside]

        def side(sign, u_shift, h_shift, v_shift, start, u_start):
            far = [pr[sign, g, strided(j)] - ps[1 - sign, g, strided(j)] for j in range(6)]

            def cut(shift, first, width):
                where = (place >= first) & (place < first + width)
                return [jnp.where(where, pltpu.roll(w, shift % COLS, 1) if shift else w, 0.0) for w in far]

            return cut(h_shift, start, 5), cut(u_shift, u_start, 6), cut(v_shift, start, 5)

        left = side(0, 0, -5, -10, 1, 0)
        right = side(1, 6, 0, -5, 6, 6)
        out = advance(*[p + w for p, w in zip(left, right)], keep)
        for k in range(3):
            for j in range(6):
                strip[k, j] = jnp.where(place < 6, out[k][6 + j], out[k][j])

    def forecast(first, s, count):
        out = advance(
            *[[x[k, first + t, strided(j)] for t in range(count) for j in range(6)] for k in range(3)], inside
        )
        for t in range(count):
            shift = (2 * COLS - 6 - 16 * (s + t)) % COLS
            for k in range(3):
                for j in range(6):
                    more = jnp.where(edge, pltpu.roll(strip[k, j], shift, 1), 0.0)
                    f[k, first + t, strided(j)] = out[k][6 * t + j] + more

    halo_wait(NHALO, True)
    strips(MEAN // 8)
    forecast(MEAN, 0, 1)
    mean = [f[k, MEAN, OWN] for k in range(3)]
    for k in range(3):
        state[k] = mean[k]
    obs_weight = obs_mask[...].astype(F32) * obs_precision[...]

    def set_coefficients(sh, su, sv):
        residual = obs_weight * (obs_value[...] - sh - 0.15 * (su * su + sv * sv))
        coef[0] = residual
        coef[1] = 0.3 * su * residual
        coef[2] = 0.3 * sv * residual

    set_coefficients(*mean)

    def row_copy(it, k, n):
        members = pl.ds(n * CHUNK, CHUNK)
        return pltpu.make_async_remote_copy(
            src_ref=c.at[members], dst_ref=rc.at[it, 1 - k, members],
            send_sem=row_ss.at[it, k, n], recv_sem=row_rs.at[it, k, n],
            device_id=near[k], device_id_type=MESH,
        )

    def by_relay(k, n):
        return (m == (8 if k == 0 else 7)) & (lax.rem(n, 2) == 1)

    def at_relay(k, n):
        return (m == (0 if k == 0 else NMEM - 1)) & (lax.rem(n, 2) == 1)

    def relay_in(it, k, n):
        return pltpu.make_async_remote_copy(
            src_ref=c.at[pl.ds(n * CHUNK, CHUNK)], dst_ref=relay.at[it, n // 2],
            send_sem=row_ss.at[it, k, n], recv_sem=relay_rs.at[it, n // 2],
            device_id=(0 if k == 0 else NMEM - 1, b), device_id_type=MESH,
        )

    def relay_out(it, k, n):
        return pltpu.make_async_remote_copy(
            src_ref=relay.at[it, n // 2], dst_ref=rc.at[it, 1 - k, pl.ds(n * CHUNK, CHUNK)],
            send_sem=row_ss.at[it, k, n], recv_sem=row_rs.at[it, k, n],
            device_id=(7 if k == 0 else 8, b), device_id_type=MESH,
        )

    def row_start(it, n):
        for k, there in ((0, has_up), (1, has_dn)):
            pl.when(there & jnp.logical_not(by_relay(k, n)))(row_copy(it, k, n).start)
            pl.when(by_relay(k, n))(relay_in(it, k, n).start)

    def relay_forward(it, n):
        for k in range(2):

            @pl.when(at_relay(k, n))
            def _(k=k):
                relay_in(it, k, n).wait_recv()
                relay_out(it, k, n).start()

    def row_wait(it, n):
        @pl.when(has_up)
        def _():
            row_copy(it, 1, n).wait_recv()

        @pl.when(has_dn)
        def _():
            row_copy(it, 0, n).wait_recv()

    def row_sent(it, n):
        for k, there in ((0, has_up), (1, has_dn)):
            pl.when(there | at_relay(k, n))(row_copy(it, k, n).wait_send)

    def col_copy(it, k, n):
        quads = pl.ds(n * QUADS, QUADS)
        return pltpu.make_async_remote_copy(
            src_ref=ls.at[k, quads], dst_ref=lr.at[it, 1 - k, quads],
            send_sem=col_ss.at[it, k, n], recv_sem=col_rs.at[it, k, n],
            device_id=near[2 + k], device_id_type=MESH,
        )

    scale = 1.0 / math.sqrt(MEMBERS - 1.0)

    def first_chunk(n, carry):
        halo_wait(n)
        for gg in range(2):
            g = n * 2 + gg
            strips(g)

            for s in range(0, 8, TOGETHER):
                first = g * 8 + s
                forecast(first, s, TOGETHER)
                for t in range(TOGETHER):
                    i = first + t
                    total = None
                    for k in range(3):
                        anomaly = (f[k, i, OWN] - state[k]) * scale
                        x[k, i, OWN] = anomaly
                        term = anomaly * coef[k]
                        total = term if total is None else total + term
                    c[i] = total
            row_start(0, g)
        return carry

    lax.fori_loop(0, NHALO, first_chunk, 0)

    stores = [
        pltpu.make_async_copy(f.at[k, pl.ds(0, MEMBERS), OWN], dst, store_sem.at[k])
        for k, dst in enumerate((h_out, u_out, v_out))
    ]
    for copy in stores:
        copy.start()

    def taper_rows(it, n):
        relay_forward(it, n)
        row_wait(it, n)

        for qq in range(QUADS):
            q = n * QUADS + qq
            parts_high, parts_low = [], []
            for ref_part in range(3):
                wide = []
                for s in range(4):
                    i = q * 4 + s
                    wide.append(rc[it, 0, i] if ref_part == 0 else (c[i] if ref_part == 1 else rc[it, 1, i]))
                high, low = split(jnp.concatenate(wide, axis=1))
                parts_high.append(high)
                parts_low.append(low)
            right_side = jnp.concatenate(parts_high + parts_low, axis=0)
            both = jnp.dot(lat_k[...], right_side, preferred_element_type=F32)
            lat = both[:32] + both[32:]
            to_left = jnp.zeros((ROWS, COLS), F32)
            to_right = jnp.zeros((ROWS, COLS), F32)
            for s in range(4):
                part = lat[:, s * COLS:(s + 1) * COLS]
                lt[s, q] = part
                where = (lane >= 32 * s) & (lane < 32 * s + 32)
                to_left = jnp.where(where, pltpu.roll(part, 32 * s, 1) if s else part, to_left)
                to_right = jnp.where(where, pltpu.roll(part, 32 * s + 32, 1) if s < 3 else part, to_right)
            ls[0, q] = to_left
            ls[1, q] = to_right

        for k in range(2):
            col_copy(it, k, n).start()

    def taper_cols(it, n, factor):
        for k in range(2):
            col_copy(it, k, n).wait_recv()
        quads = pl.ds(n * QUADS, QUADS)
        size = QUADS * ROWS
        lh, ll = split(lr[it, 0, quads].reshape(size, COLS))
        rhh, rl = split(lr[it, 1, quads].reshape(size, COLS))
        totals = [None] * 4
        for s in range(4):
            mh, ml = split(lt[s, quads].reshape(size, COLS))
            a = jnp.dot(jnp.concatenate([mh, lh, rhh], axis=1), lon_k[s], preferred_element_type=F32)
            d = jnp.dot(jnp.concatenate([ml, ll, rl], axis=1), lon_k[s, :, pl.ds(0, 128)], preferred_element_type=F32)
            g = (a[:, :COLS] + a[:, COLS:] + d).reshape(QUADS, ROWS, COLS)
            if it == 0:
                g1[s, quads] = g
            else:
                g = factor * g1[s, quads] - g
            for qq in range(QUADS):
                i = (n * QUADS + qq) * 4 + s
                part = g[qq]
                terms = [x[k, i, OWN] * part for k in range(3)] + [part * part]
                totals = [t if o is None else o + t for o, t in zip(totals, terms)]
        for k in range(3):
            s_acc[it, k] += totals[k]
        sq[...] += totals[3]

    def localize(it, factor):
        def body(n, carry):
            @pl.when(n < NCHUNK)
            def _():
                taper_rows(it, n)

            @pl.when(n >= SKEW)
            def _():
                taper_cols(it, n - SKEW, factor)

            return carry

        lax.fori_loop(0, NCHUNK + SKEW, body, 0)

    def sum_all(it):
        value = sq[...]
        value = value[:8] + value[8:16] + value[16:24] + value[24:]
        slot = 0
        for stage in stages:
            red[it, slot] = value
            copies = [
                pltpu.make_async_remote_copy(
                    src_ref=red.at[it, slot], dst_ref=red.at[it, slot + 1 + j],
                    send_sem=red_ss.at[it, slot + j], recv_sem=red_rs.at[it, slot + j],
                    device_id=d, device_id_type=MESH,
                )
                for j, d in enumerate(stage)
            ]
            for copy in copies:
                copy.start()
            for copy in copies:
                copy.wait_recv()
            for j in range(len(stage)):
                value = value + red[it, slot + 1 + j]
            for copy in copies:
                copy.wait_send()
            slot += 1 + len(stage)
        total = jnp.sum(jnp.sum(value, axis=0, keepdims=True), axis=1, keepdims=True)
        return steps[it].astype(F32) / 64.0 / jnp.sqrt(total / CELLS + 1e-6)

    for it in range(2):
        for k in range(3):
            s_acc[it, k] = jnp.zeros((ROWS, COLS), F32)
    sq[...] = jnp.zeros((ROWS, COLS), F32)
    localize(0, None)
    factor1 = sum_all(0)

    def sent(n, carry):
        row_sent(0, n)
        for k in range(2):
            col_copy(0, k, n).wait_send()
        return carry

    lax.fori_loop(0, NCHUNK, sent, 0)
    sq[...] = jnp.zeros((ROWS, COLS), F32)
    set_coefficients(*[state[k] + factor1 * s_acc[0, k] for k in range(3)])

    def second_chunk(n, carry):
        def one(j, carry2):
            i = n * CHUNK + j
            c[i] = x[0, i, OWN] * coef[0] + x[1, i, OWN] * coef[1] + x[2, i, OWN] * coef[2]
            return carry2

        lax.fori_loop(0, CHUNK, one, 0, unroll=4)
        row_start(1, n)
        return carry

    lax.fori_loop(0, NCHUNK, second_chunk, 0)
    localize(1, factor1)
    factor2 = sum_all(1)
    for k in range(3):
        inc[k] = factor1 * s_acc[0, k] - factor2 * s_acc[1, k]

    def sent2(n, carry):
        row_sent(1, n)
        for k in range(2):
            col_copy(1, k, n).wait_send()
        return carry

    lax.fori_loop(0, NCHUNK, sent2, 0)
    for copy in stores:
        copy.wait()


def per_device(height, east, north, obs_value, obs_mask, obs_precision, step_sizes):
    block = (MEMBERS, ROWS, COLS)
    vmem = pl.BlockSpec(memory_space=pltpu.VMEM)
    anyspace = pl.BlockSpec(memory_space=pl.ANY)
    dma = pltpu.SemaphoreType.DMA
    h, u, v, inc = pl.pallas_call(
        kernel,
        name="analysis",
        out_shape=[jax.ShapeDtypeStruct(block, F32)] * 3 + [jax.ShapeDtypeStruct((3, ROWS, COLS), F32)],
        in_specs=[pl.BlockSpec(memory_space=pltpu.HBM)] * 7,
        out_specs=[anyspace] * 3 + [vmem],
        scratch_shapes=[
            pltpu.VMEM((3, MEMBERS + 8, 48, COLS), F32),
            pltpu.VMEM((3, MEMBERS + 1, 48, COLS), F32),
            pltpu.VMEM((2, GROUPS, 48, COLS), F32),
            pltpu.VMEM((2, GROUPS, 48, COLS), F32),
            pltpu.VMEM(block, F32),
            pltpu.VMEM((2, 2) + block, F32),
            pltpu.VMEM((4, MEMBERS // 4, ROWS, COLS), F32),
            pltpu.VMEM((2, MEMBERS // 4, ROWS, COLS), F32),
            pltpu.VMEM((2, 2, MEMBERS // 4, ROWS, COLS), F32),
            pltpu.VMEM((4, MEMBERS // 4, ROWS, COLS), F32),
            pltpu.VMEM((64, 192), BF16),
            pltpu.VMEM((4, 384, 256), BF16),
            pltpu.VMEM((3, ROWS, COLS), F32),
            pltpu.VMEM((3, ROWS, COLS), F32),
            pltpu.VMEM((2, 3, ROWS, COLS), F32),
            pltpu.VMEM((ROWS, COLS), F32),
            pltpu.VMEM((2, 14, 8, COLS), F32),
            pltpu.VMEM((ROWS, COLS), F32),
            pltpu.VMEM((ROWS, COLS), jnp.int32),
            pltpu.VMEM((ROWS, COLS), F32),
            pltpu.SMEM((2,), jnp.int32),
            pltpu.VMEM((3, 6, 8, COLS), F32),
            pltpu.VMEM((2, NCHUNK // 2, CHUNK, ROWS, COLS), F32),
            dma((7,)), dma((3,)),
            dma((NHALO + 1, 10)), dma((NHALO + 1, 10)),
            dma((2, 2, NCHUNK)), dma((2, 2, NCHUNK)), dma((2, NCHUNK // 2)),
            dma((2, 2, NCHUNK)), dma((2, 2, NCHUNK)),
            dma((2, 14)), dma((2, 14)),
        ],
        compiler_params=pltpu.CompilerParams(
            collective_id=0, has_side_effects=True, vmem_limit_bytes=48 << 20
        ),
    )(height, east, north, obs_value, obs_mask, obs_precision, step_sizes)
    return h + inc[0], u + inc[1], v + inc[2]


def solution(mesh):
    spec3 = P(None, "member", "band")
    spec2 = P("member", "band")
    return jax.shard_map(
        per_device,
        mesh=mesh,
        in_specs=(spec3, spec3, spec3, spec2, spec2, spec2, P()),
        out_specs=(spec3, spec3, spec3),
        check_vma=False,
    )
```

time: 170 us -> 129 us (0.76)
  Pallas kernels: 162 us -> 120 us
    pallas_call x1, Pallas kernels: 162 us -> 120 us  [per_device(): pl.pallas_call(kernel, name='analysis', out_shape=[jax.ShapeDtypeStruct(b...]
where the time goes in v2:
time: 129 us; the launch traced here: 128 us
  Pallas kernels  120 us (93%)
  local copies, waits for them, and re-layouts  4.12 us (3%)
  other arithmetic  2.97 us (2%)
    pallas_call x1, Pallas kernels, per_device(): pl.pallas_call(kernel, name='analysis', out_shape=[jax.ShapeDtypeStruct(b...  120 us
    unnamed x10, local copies, waits for them, and re-layouts  4.11 us
    add x2, other arithmetic, per_device(): return (h + inc[0], u + inc[1], v + inc[2])  2.97 us

profile of v2, /device:TPU:0, one launch (start us, length us, event | category | flops | bytes accessed | tf_op | source)
XLA Modules:
  0.0 128.0 jit_solution(450665926217994495)
XLA Ops:
  0.6 0.0 copy-start
  0.6 1.3 %copy-done = f32[80,32,128]{2,1,0:T(8,128)S(1)} copy-done((f32[80,32,128]{2,1,0:T(8,128)S(1)}, f32[80,32,128]{2,1,0:T(8,128)}, u32[]{:S(2)}) %copy-start) | copy-done | bytes 1310744
  1.9 0.0 copy-start.1
  2.0 0.7 copy-done.1
  2.7 0.0 copy-start.2
  2.7 0.7 copy-done.2
  3.4 0.0 copy-start.3
  3.4 0.7 copy-done.3
  4.1 0.0 copy-start.4
  4.1 0.7 copy-done.4
  4.8 120.2 %analysis.1 = (f32[80,32,128]{2,1,0:T(8,128)S(1)}, f32[80,32,128]{2,1,0:T(8,128)S(1)}, f32[80,32,128]{2,1,0:T(8,128)S(1)}, f32[3,32,128]{2,1,0:T(8,128)S(1)}) custom-call(f32[80,32,128]{2,1,0:T(8,128)S(1)} %copy-done, f32[80,32,128]{2,1,0:T(8,128)} %u_in.1, f32[80,32,128]{2,1,0:T(8,128)} %v_in.1, f32[32,128]{1,0:T(8,128)S(1)} %copy-done.1, ...), custom_call_target="tpu_custom_call" | custom-call | tf_op jit(solution)/shard_map/analysis/pallas_call | solution.py:558
  125.0 1.2 broadcast_add_fusion.2
  126.2 1.8 %broadcast_add_fusion = (f32[80,32,128]{2,1,0:T(8,128)}, f32[80,32,128]{2,1,0:T(8,128)}) fusion(f32[80,32,128]{2,1,0:T(8,128)S(1)} %get-tuple-element.10, f32[32,128]{1,0:T(8,128)S(1)} %get-tuple-element.11, f32[80,32,128]{2,1,0:T(8,128)S(1)} %get-tuple-element.9, f32[32,128]{1,0:T(8,128)S(1)} %get-tuple-element.12), kind=kLoop, calls=%fused_computation | loop fusion | flops 655360 | bytes 5275648 | tf_op jit(solution)/shard_map/add | solution.py:598
  (1 shorter events, 0.0 us)
Async XLA Ops:
  0.6 1.3 %copy-start = (f32[80,32,128]{2,1,0:T(8,128)S(1)}, f32[80,32,128]{2,1,0:T(8,128)}, u32[]{:S(2)}) copy-start(f32[80,32,128]{2,1,0:T(8,128)} %h_in.1) | copy-start | bytes 3932164
  1.9 0.7 copy-start.1
  2.7 0.7 copy-start.2
  3.4 0.7 copy-start.3
  4.1 0.7 copy-start.4

commit v3 on v2

--- a/solution.py
+++ b/solution.py
@@ -73,11 +73,11 @@
 
 
 def kernel(
-    h_in, u_in, v_in, value_in, mask_in, precision_in, steps_in,
+    h_in, u_in, v_in, observed_in,
     h_out, u_out, v_out, inc,
     x, f, ps, pr, c, rc, lt, ls, lr, g1, lat_k, lon_k, coef, state, s_acc, sq, red,
-    obs_value, obs_mask, obs_precision, steps, strip, relay,
-    load_sem, store_sem, halo_ss, halo_rs, row_ss, row_rs, relay_rs, col_ss, col_rs, red_ss, red_rs,
+    observed, strip, relay, relay_x, relay_p,
+    load_sem, store_sem, halo_ss, halo_rs, halo_relay_rs, row_ss, row_rs, relay_rs, col_ss, col_rs, red_ss, red_rs,
 ):
     m = lax.axis_index("member")
     b = lax.axis_index("band")
@@ -117,10 +117,7 @@
             (h_in, x.at[0, pl.ds(0, MEMBERS), OWN]),
             (u_in, x.at[1, pl.ds(0, MEMBERS), OWN]),
             (v_in, x.at[2, pl.ds(0, MEMBERS), OWN]),
-            (value_in, obs_value),
-            (mask_in, obs_mask),
-            (precision_in, obs_precision),
-            (steps_in, steps),
+            (observed_in, observed),
         ))
     ]
     for copy in loads:
@@ -162,19 +159,58 @@
             device_id=to, device_id_type=MESH,
         )
 
+    def halo_relay_in(k, n):
+        part = k % 4
+        return pltpu.make_async_remote_copy(
+            src_ref=(x.at[:, pl.ds(n * 16, 16), TOP if k < 4 else BOTTOM] if part == 0
+                     else ps.at[:, pl.ds(n * 2, 2), TOP if k < 4 else BOTTOM]),
+            dst_ref=(relay_x if part == 0 else relay_p).at[n // 2],
+            send_sem=halo_ss.at[n, k], recv_sem=halo_relay_rs.at[n // 2, part],
+            device_id=(0 if k < 4 else NMEM - 1, b), device_id_type=MESH,
+        )
+
+    def halo_relay_out(k, n):
+        part = k % 4
+        rows = BELOW if k < 4 else ABOVE
+        return pltpu.make_async_remote_copy(
+            src_ref=(relay_x if part == 0 else relay_p).at[n // 2],
+            dst_ref=x.at[:, pl.ds(n * 16, 16), rows] if part == 0 else ps.at[:, pl.ds(n * 2, 2), rows],
+            send_sem=halo_ss.at[n, k], recv_sem=halo_rs.at[n, k],
+            device_id=(7 if k < 4 else 8, b), device_id_type=MESH,
+        )
+
+    def halo_forward(n):
+        for end, ks in ((0, (0, 1)), (NMEM - 1, (4, 5))):
+
+            @pl.when((m == end) & (lax.rem(n, 2) == 1))
+            def _(ks=ks):
+                for k in ks:
+                    halo_relay_in(k, n).wait_recv()
+                    halo_relay_out(k, n).start()
+
     def halo_start(n, mean=False):
         for k in (8, 9):
             halo_copy(k, n, mean).start()
-
-        @pl.when(has_up)
-        def _():
-            for k in range(0, 4):
-                halo_copy(k, n, mean).start()
-
-        @pl.when(has_dn)
-        def _():
-            for k in range(4, 8):
-                halo_copy(k, n, mean).start()
+        odd = False if mean else lax.rem(n, 2) == 1
+        for there, source, ks in ((has_up, 8, range(0, 4)), (has_dn, 7, range(4, 8))):
+            away = (m == source) & odd
+
+            @pl.when(there & jnp.logical_not(away))
+            def _(ks=ks):
+                for k in ks[:2]:
+                    halo_copy(k, n, mean).start()
+
+            if not mean:
+
+                @pl.when(away)
+                def _(ks=ks):
+                    for k in ks[:2]:
+                        halo_relay_in(k, n).start()
+
+            @pl.when(there)
+            def _(ks=ks):
+                for k in ks[2:]:
+                    halo_copy(k, n, mean).start()
 
     def halo_wait(n, mean=False):
         @pl.when(has_up)
@@ -194,6 +230,14 @@
         for k in (8, 9):
             halo_copy(k, n, mean).wait_recv()
             halo_copy(k, n, mean).wait_send()
+
+        if not mean:
+            for end, ks in ((0, (0, 1)), (NMEM - 1, (4, 5))):
+
+                @pl.when((m == end) & (lax.rem(n, 2) == 1))
+                def _(ks=ks):
+                    for k in ks:
+                        halo_relay_out(k, n).wait_send()
 
     def send_halo(n, carry):
         for gg in range(2):
@@ -304,10 +348,9 @@
     mean = [f[k, MEAN, OWN] for k in range(3)]
     for k in range(3):
         state[k] = mean[k]
-    obs_weight = obs_mask[...].astype(F32) * obs_precision[...]
 
     def set_coefficients(sh, su, sv):
-        residual = obs_weight * (obs_value[...] - sh - 0.15 * (su * su + sv * sv))
+        residual = observed[pl.ds(ROWS, ROWS)] * (observed[pl.ds(0, ROWS)] - sh - 0.15 * (su * su + sv * sv))
         coef[0] = residual
         coef[1] = 0.3 * su * residual
         coef[2] = 0.3 * sv * residual
@@ -380,6 +423,7 @@
 
     def first_chunk(n, carry):
         halo_wait(n)
+        pl.when(n + 1 < NHALO)(lambda: halo_forward(n + 1))
         for gg in range(2):
             g = n * 2 + gg
             strips(g)
@@ -504,7 +548,7 @@
                 copy.wait_send()
             slot += 1 + len(stage)
         total = jnp.sum(jnp.sum(value, axis=0, keepdims=True), axis=1, keepdims=True)
-        return steps[it].astype(F32) / 64.0 / jnp.sqrt(total / CELLS + 1e-6)
+        return observed[pl.ds(2 * ROWS + 8 * it, 1), pl.ds(0, 1)] / jnp.sqrt(total / CELLS + 1e-6)
 
     for it in range(2):
         for k in range(3):
@@ -555,11 +599,15 @@
     vmem = pl.BlockSpec(memory_space=pltpu.VMEM)
     anyspace = pl.BlockSpec(memory_space=pl.ANY)
     dma = pltpu.SemaphoreType.DMA
+    steps = jnp.broadcast_to((step_sizes.astype(F32) / 64.0)[:, None, None], (2, 8, COLS))
+    observed = jnp.concatenate(
+        [obs_value, obs_mask.astype(F32) * obs_precision, steps.reshape(16, COLS)], axis=0
+    )
     h, u, v, inc = pl.pallas_call(
         kernel,
         name="analysis",
         out_shape=[jax.ShapeDtypeStruct(block, F32)] * 3 + [jax.ShapeDtypeStruct((3, ROWS, COLS), F32)],
-        in_specs=[pl.BlockSpec(memory_space=pltpu.HBM)] * 7,
+        in_specs=[pl.BlockSpec(memory_space=pltpu.HBM)] * 4,
         out_specs=[anyspace] * 3 + [vmem],
         scratch_shapes=[
             pltpu.VMEM((3, MEMBERS + 8, 48, COLS), F32),
@@ -579,22 +627,21 @@
             pltpu.VMEM((2, 3, ROWS, COLS), F32),
             pltpu.VMEM((ROWS, COLS), F32),
             pltpu.VMEM((2, 14, 8, COLS), F32),
-            pltpu.VMEM((ROWS, COLS), F32),
-            pltpu.VMEM((ROWS, COLS), jnp.int32),
-            pltpu.VMEM((ROWS, COLS), F32),
-            pltpu.SMEM((2,), jnp.int32),
+            pltpu.VMEM((2 * ROWS + 16, COLS), F32),
             pltpu.VMEM((3, 6, 8, COLS), F32),
             pltpu.VMEM((2, NCHUNK // 2, CHUNK, ROWS, COLS), F32),
-            dma((7,)), dma((3,)),
-            dma((NHALO + 1, 10)), dma((NHALO + 1, 10)),
+            pltpu.VMEM((NHALO // 2, 3, 16, 8, COLS), F32),
+            pltpu.VMEM((NHALO // 2, 2, 2, 8, COLS), F32),
+            dma((4,)), dma((3,)),
+            dma((NHALO + 1, 10)), dma((NHALO + 1, 10)), dma((NHALO // 2, 2)),
             dma((2, 2, NCHUNK)), dma((2, 2, NCHUNK)), dma((2, NCHUNK // 2)),
             dma((2, 2, NCHUNK)), dma((2, 2, NCHUNK)),
             dma((2, 14)), dma((2, 14)),
         ],
         compiler_params=pltpu.CompilerParams(
-            collective_id=0, has_side_effects=True, vmem_limit_bytes=48 << 20
+            collective_id=0, has_side_effects=True, vmem_limit_bytes=50 << 20
         ),
-    )(height, east, north, obs_value, obs_mask, obs_precision, step_sizes)
+    )(height, east, north, observed)
     return h + inc[0], u + inc[1], v + inc[2]
 
 

time: 129 us -> 120 us (0.930)
  Pallas kernels: 120 us -> 113 us
  local copies, waits for them, and re-layouts: 4.12 us -> 0.24 us
  other arithmetic: 2.97 us -> 5.15 us
    pallas_call x1, Pallas kernels: 120 us -> 113 us  [per_device(): pl.pallas_call(kernel, name='analysis', out_shape=[jax.ShapeDtypeStruct(b...]
    unnamed x10 -> x0, local copies, waits for them, and re-layouts: 4.11 us -> none
where the time goes in v3:
time: 120 us; the launch traced here: 119 us
  Pallas kernels  113 us (94%)
  other arithmetic  5.15 us (4%)
    pallas_call x1, Pallas kernels, per_device(): pl.pallas_call(kernel, name='analysis', out_shape=[jax.ShapeDtypeStruct(b...  113 us
    add x2, other arithmetic, per_device(): return (h + inc[0], u + inc[1], v + inc[2])  2.96 us

profile of v3, /device:TPU:0, one launch (start us, length us, event | category | flops | bytes accessed | tf_op | source)
XLA Modules:
  0.0 119.0 jit_solution(9898926244582404344)
XLA Ops:
  0.6 0.7 convert_multiply_fusion.1
  1.3 0.1 broadcast_in_dim.10
  1.4 0.1 reshape.9
  1.4 0.1 pad.2.clone
  1.5 0.7 convert_multiply_fusion
  2.3 0.8 maximum_maximum_fusion.observed_in
  3.1 112.9 %analysis.1 = (f32[80,32,128]{2,1,0:T(8,128)S(1)}, f32[80,32,128]{2,1,0:T(8,128)S(1)}, f32[80,32,128]{2,1,0:T(8,128)S(1)}, f32[3,32,128]{2,1,0:T(8,128)S(1)}) custom-call(f32[80,32,128]{2,1,0:T(8,128)} %h_in.1, f32[80,32,128]{2,1,0:T(8,128)} %u_in.1, f32[80,32,128]{2,1,0:T(8,128)} %v_in.1, f32[80,128]{1,0:T(8,128)S(1)} %maximum_maximum_fusion.observed_in), custom_call_target="tpu_custom_call" | custom-call | tf_op jit(solution)/shard_map/analysis/pallas_call | solution.py:606
  116.0 1.2 broadcast_add_fusion.2
  117.2 1.8 %broadcast_add_fusion = (f32[80,32,128]{2,1,0:T(8,128)}, f32[80,32,128]{2,1,0:T(8,128)}) fusion(f32[80,32,128]{2,1,0:T(8,128)S(1)} %get-tuple-element.10, f32[32,128]{1,0:T(8,128)S(1)} %get-tuple-element.11, f32[80,32,128]{2,1,0:T(8,128)S(1)} %get-tuple-element.9, f32[32,128]{1,0:T(8,128)S(1)} %get-tuple-element.12), kind=kLoop, calls=%fused_computation | loop fusion | flops 655360 | bytes 5275648 | tf_op jit(solution)/shard_map/add | solution.py:645
  (1 shorter events, 0.0 us)

commit v4 on v3

--- a/solution.py
+++ b/solution.py
@@ -27,9 +27,11 @@
 QUADS = CHUNK // 4
 NHALO = MEMBERS // 16
 SKEW = 5
+LAG = 3
+BEHIND = 5
 TOGETHER = 8
-ABOVE, OWN, BELOW = pl.ds(0, 8), pl.ds(8, 32), pl.ds(40, 8)
-TOP, BOTTOM = pl.ds(8, 8), pl.ds(32, 8)
+ABOVE, OWN, BELOW = pl.ds(2, 6), pl.ds(8, 32), pl.ds(40, 6)
+TOP, BOTTOM = pl.ds(8, 6), pl.ds(34, 6)
 CELLS = float(MEMBERS * 512 * 1024)
 
 
@@ -262,9 +264,9 @@
     lax.fori_loop(1, NHALO, send_halo, 0)
 
     def clear(halo, side):
-        x[:, :, halo, :] = jnp.zeros((3, MEMBERS + 8, 8, COLS), F32)
-        ps[:, :, halo, :] = jnp.zeros((2, GROUPS, 8, COLS), F32)
-        pr[:, :, halo, :] = jnp.zeros((2, GROUPS, 8, COLS), F32)
+        x[:, :, halo, :] = jnp.zeros((3, MEMBERS + 8, 6, COLS), F32)
+        ps[:, :, halo, :] = jnp.zeros((2, GROUPS, 6, COLS), F32)
+        pr[:, :, halo, :] = jnp.zeros((2, GROUPS, 6, COLS), F32)
         for it in range(2):
             rc[it, side] = jnp.zeros((MEMBERS, ROWS, COLS), F32)
 
@@ -420,37 +422,6 @@
         )
 
     scale = 1.0 / math.sqrt(MEMBERS - 1.0)
-
-    def first_chunk(n, carry):
-        halo_wait(n)
-        pl.when(n + 1 < NHALO)(lambda: halo_forward(n + 1))
-        for gg in range(2):
-            g = n * 2 + gg
-            strips(g)
-
-            for s in range(0, 8, TOGETHER):
-                first = g * 8 + s
-                forecast(first, s, TOGETHER)
-                for t in range(TOGETHER):
-                    i = first + t
-                    total = None
-                    for k in range(3):
-                        anomaly = (f[k, i, OWN] - state[k]) * scale
-                        x[k, i, OWN] = anomaly
-                        term = anomaly * coef[k]
-                        total = term if total is None else total + term
-                    c[i] = total
-            row_start(0, g)
-        return carry
-
-    lax.fori_loop(0, NHALO, first_chunk, 0)
-
-    stores = [
-        pltpu.make_async_copy(f.at[k, pl.ds(0, MEMBERS), OWN], dst, store_sem.at[k])
-        for k, dst in enumerate((h_out, u_out, v_out))
-    ]
-    for copy in stores:
-        copy.start()
 
     def taper_rows(it, n):
         relay_forward(it, n)
@@ -483,6 +454,43 @@
 
         for k in range(2):
             col_copy(it, k, n).start()
+
+    def first_chunk(n, carry):
+        halo_wait(n)
+        pl.when(n + 1 < NHALO)(lambda: halo_forward(n + 1))
+        for gg in range(2):
+            g = n * 2 + gg
+            strips(g)
+
+            for s in range(0, 8, TOGETHER):
+                first = g * 8 + s
+                forecast(first, s, TOGETHER)
+                for t in range(TOGETHER):
+                    i = first + t
+                    total = None
+                    for k in range(3):
+                        anomaly = (f[k, i, OWN] - state[k]) * scale
+                        x[k, i, OWN] = anomaly
+                        term = anomaly * coef[k]
+                        total = term if total is None else total + term
+                    c[i] = total
+            row_start(0, g)
+
+        @pl.when(n >= LAG)
+        def _():
+            for gg in range(2):
+                taper_rows(0, 2 * (n - LAG) + gg)
+
+        return carry
+
+    lax.fori_loop(0, NHALO, first_chunk, 0)
+
+    stores = [
+        pltpu.make_async_copy(f.at[k, pl.ds(0, MEMBERS), OWN], dst, store_sem.at[k])
+        for k, dst in enumerate((h_out, u_out, v_out))
+    ]
+    for copy in stores:
+        copy.start()
 
     def taper_cols(it, n, factor):
         for k in range(2):
@@ -511,23 +519,26 @@
         sq[...] += totals[3]
 
     def localize(it, factor):
+        early, behind = (NCHUNK - 2 * LAG, BEHIND) if it == 0 else (0, SKEW)
+
         def body(n, carry):
-            @pl.when(n < NCHUNK)
+            @pl.when(n + early < NCHUNK)
             def _():
-                taper_rows(it, n)
-
-            @pl.when(n >= SKEW)
+                taper_rows(it, n + early)
+
+            @pl.when(n >= behind)
             def _():
-                taper_cols(it, n - SKEW, factor)
+                taper_cols(it, n - behind, factor)
 
             return carry
 
-        lax.fori_loop(0, NCHUNK + SKEW, body, 0)
+        lax.fori_loop(0, NCHUNK + behind, body, 0)
 
     def sum_all(it):
         value = sq[...]
         value = value[:8] + value[8:16] + value[16:24] + value[24:]
         slot = 0
+        started = []
         for stage in stages:
             red[it, slot] = value
             copies = [
@@ -544,9 +555,10 @@
                 copy.wait_recv()
             for j in range(len(stage)):
                 value = value + red[it, slot + 1 + j]
-            for copy in copies:
-                copy.wait_send()
+            started.extend(copies)
             slot += 1 + len(stage)
+        for copy in started:
+            copy.wait_send()
         total = jnp.sum(jnp.sum(value, axis=0, keepdims=True), axis=1, keepdims=True)
         return observed[pl.ds(2 * ROWS + 8 * it, 1), pl.ds(0, 1)] / jnp.sqrt(total / CELLS + 1e-6)
 
@@ -630,8 +642,8 @@
             pltpu.VMEM((2 * ROWS + 16, COLS), F32),
             pltpu.VMEM((3, 6, 8, COLS), F32),
             pltpu.VMEM((2, NCHUNK // 2, CHUNK, ROWS, COLS), F32),
-            pltpu.VMEM((NHALO // 2, 3, 16, 8, COLS), F32),
-            pltpu.VMEM((NHALO // 2, 2, 2, 8, COLS), F32),
+            pltpu.VMEM((NHALO // 2, 3, 16, 6, COLS), F32),
+            pltpu.VMEM((NHALO // 2, 2, 2, 6, COLS), F32),
             dma((4,)), dma((3,)),
             dma((NHALO + 1, 10)), dma((NHALO + 1, 10)), dma((NHALO // 2, 2)),
             dma((2, 2, NCHUNK)), dma((2, 2, NCHUNK)), dma((2, NCHUNK // 2)),

time: 120 us -> 114 us (0.950)
  Pallas kernels: 113 us -> 107 us
    pallas_call x1, Pallas kernels: 113 us -> 107 us  [per_device(): pl.pallas_call(kernel, name='analysis', out_shape=[jax.ShapeDtypeStruct(b...]
where the time goes in v4:
time: 114 us; the launch traced here: 113 us
  Pallas kernels  107 us (94%)
  other arithmetic  5.15 us (5%)
    pallas_call x1, Pallas kernels, per_device(): pl.pallas_call(kernel, name='analysis', out_shape=[jax.ShapeDtypeStruct(b...  107 us
    add x2, other arithmetic, per_device(): return (h + inc[0], u + inc[1], v + inc[2])  2.96 us

profile of v4, /device:TPU:0, one launch (start us, length us, event | category | flops | bytes accessed | tf_op | source)
XLA Modules:
  0.0 113.4 jit_solution(5480691738796698716)
XLA Ops:
  0.6 0.7 convert_multiply_fusion.1
  1.3 0.1 broadcast_in_dim.10
  1.4 0.1 reshape.9
  1.4 0.1 pad.2.clone
  1.5 0.7 convert_multiply_fusion
  2.3 0.8 maximum_maximum_fusion.observed_in
  3.1 107.4 %analysis.1 = (f32[80,32,128]{2,1,0:T(8,128)S(1)}, f32[80,32,128]{2,1,0:T(8,128)S(1)}, f32[80,32,128]{2,1,0:T(8,128)S(1)}, f32[3,32,128]{2,1,0:T(8,128)S(1)}) custom-call(f32[80,32,128]{2,1,0:T(8,128)} %h_in.1, f32[80,32,128]{2,1,0:T(8,128)} %u_in.1, f32[80,32,128]{2,1,0:T(8,128)} %v_in.1, f32[80,128]{1,0:T(8,128)S(1)} %maximum_maximum_fusion.observed_in), custom_call_target="tpu_custom_call" | custom-call | tf_op jit(solution)/shard_map/analysis/pallas_call | solution.py:618
  110.5 1.2 %broadcast_add_fusion.2 = f32[80,32,128]{2,1,0:T(8,128)} fusion(f32[80,32,128]{2,1,0:T(8,128)S(1)} %get-tuple-element.7, f32[32,128]{1,0:T(8,128)S(1)} %get-tuple-element.13), kind=kLoop, calls=%fused_computation.2 | loop fusion | flops 327680 | bytes 2637824 | tf_op jit(solution)/shard_map/add | solution.py:657
  111.7 1.8 %broadcast_add_fusion = (f32[80,32,128]{2,1,0:T(8,128)}, f32[80,32,128]{2,1,0:T(8,128)}) fusion(f32[80,32,128]{2,1,0:T(8,128)S(1)} %get-tuple-element.10, f32[32,128]{1,0:T(8,128)S(1)} %get-tuple-element.11, f32[80,32,128]{2,1,0:T(8,128)S(1)} %get-tuple-element.9, f32[32,128]{1,0:T(8,128)S(1)} %get-tuple-element.12), kind=kLoop, calls=%fused_computation | loop fusion | flops 655360 | bytes 5275648 | tf_op jit(solution)/shard_map/add | solution.py:657
  (1 shorter events, 0.0 us)

commit v5 on v4

--- a/solution.py
+++ b/solution.py
@@ -26,7 +26,7 @@
 NCHUNK = MEMBERS // CHUNK
 QUADS = CHUNK // 4
 NHALO = MEMBERS // 16
-SKEW = 5
+SKEW = 4
 LAG = 3
 BEHIND = 5
 TOGETHER = 8
@@ -424,8 +424,8 @@
     scale = 1.0 / math.sqrt(MEMBERS - 1.0)
 
     def taper_rows(it, n):
-        relay_forward(it, n)
         row_wait(it, n)
+        pl.when(n + 1 < NCHUNK)(lambda: relay_forward(it, n + 1))
 
         for qq in range(QUADS):
             q = n * QUADS + qq

time: 114 us -> 113 us (level)
  no operation moved by 1% of the time
where the time goes in v5:
time: 113 us; the launch traced here: 112 us
  Pallas kernels  106 us (94%)
  other arithmetic  5.15 us (5%)
    pallas_call x1, Pallas kernels, per_device(): pl.pallas_call(kernel, name='analysis', out_shape=[jax.ShapeDtypeStruct(b...  106 us
    add x2, other arithmetic, per_device(): return (h + inc[0], u + inc[1], v + inc[2])  2.96 us

profile of v5, /device:TPU:0, one launch (start us, length us, event | category | flops | bytes accessed | tf_op | source)
XLA Modules:
  0.0 112.4 jit_solution(15951561626915789689)
XLA Ops:
  0.6 0.7 convert_multiply_fusion.1
  1.3 0.1 broadcast_in_dim.10
  1.4 0.1 reshape.9
  1.4 0.1 pad.2.clone
  1.5 0.7 convert_multiply_fusion
  2.3 0.8 maximum_maximum_fusion.observed_in
  3.1 106.4 %analysis.1 = (f32[80,32,128]{2,1,0:T(8,128)S(1)}, f32[80,32,128]{2,1,0:T(8,128)S(1)}, f32[80,32,128]{2,1,0:T(8,128)S(1)}, f32[3,32,128]{2,1,0:T(8,128)S(1)}) custom-call(f32[80,32,128]{2,1,0:T(8,128)} %h_in.1, f32[80,32,128]{2,1,0:T(8,128)} %u_in.1, f32[80,32,128]{2,1,0:T(8,128)} %v_in.1, f32[80,128]{1,0:T(8,128)S(1)} %maximum_maximum_fusion.observed_in), custom_call_target="tpu_custom_call" | custom-call | tf_op jit(solution)/shard_map/analysis/pallas_call | solution.py:618
  109.5 1.2 %broadcast_add_fusion.2 = f32[80,32,128]{2,1,0:T(8,128)} fusion(f32[80,32,128]{2,1,0:T(8,128)S(1)} %get-tuple-element.7, f32[32,128]{1,0:T(8,128)S(1)} %get-tuple-element.13), kind=kLoop, calls=%fused_computation.2 | loop fusion | flops 327680 | bytes 2637824 | tf_op jit(solution)/shard_map/add | solution.py:657
  110.6 1.8 %broadcast_add_fusion = (f32[80,32,128]{2,1,0:T(8,128)}, f32[80,32,128]{2,1,0:T(8,128)}) fusion(f32[80,32,128]{2,1,0:T(8,128)S(1)} %get-tuple-element.10, f32[32,128]{1,0:T(8,128)S(1)} %get-tuple-element.11, f32[80,32,128]{2,1,0:T(8,128)S(1)} %get-tuple-element.9, f32[32,128]{1,0:T(8,128)S(1)} %get-tuple-element.12), kind=kLoop, calls=%fused_computation | loop fusion | flops 655360 | bytes 5275648 | tf_op jit(solution)/shard_map/add | solution.py:657
  (1 shorter events, 0.0 us)

commit v6 on v5

--- a/solution.py
+++ b/solution.py
@@ -101,9 +101,9 @@
 
     stages = [
         [at(1 - core, y, xx, z)],
-        [at(core, lax.rem(y + j, 4), xx, z) for j in (1, 2, 3)],
-        [at(core, y, lax.rem(xx + j, 4), z) for j in (1, 2, 3)],
-        [at(core, y, xx, lax.rem(z + j, 4)) for j in (1, 2, 3)],
+        [at(core, lax.rem(y + j, 4), xx, z) for j in (2, 1, 3)],
+        [at(core, y, lax.rem(xx + j, 4), z) for j in (2, 1, 3)],
+        [at(core, y, xx, lax.rem(z + j, 4)) for j in (2, 1, 3)],
     ]
 
     near = [(up, b), (dn, b), (m, lf), (m, rt), (up, lf), (up, rt), (dn, lf), (dn, rt)]
@@ -191,8 +191,6 @@
                     halo_relay_out(k, n).start()
 
     def halo_start(n, mean=False):
-        for k in (8, 9):
-            halo_copy(k, n, mean).start()
         odd = False if mean else lax.rem(n, 2) == 1
         for there, source, ks in ((has_up, 8, range(0, 4)), (has_dn, 7, range(4, 8))):
             away = (m == source) & odd
@@ -213,6 +211,9 @@
             def _(ks=ks):
                 for k in ks[2:]:
                     halo_copy(k, n, mean).start()
+
+        for k in (8, 9):
+            halo_copy(k, n, mean).start()
 
     def halo_wait(n, mean=False):
         @pl.when(has_up)

time: 113 us -> 113 us (level)
  no operation moved by 1% of the time
where the time goes in v6:
time: 113 us; the launch traced here: 112 us
  Pallas kernels  106 us (94%)
  other arithmetic  5.15 us (5%)
    pallas_call x1, Pallas kernels, per_device(): pl.pallas_call(kernel, name='analysis', out_shape=[jax.ShapeDtypeStruct(b...  106 us
    add x2, other arithmetic, per_device(): return (h + inc[0], u + inc[1], v + inc[2])  2.96 us

profile of v6, /device:TPU:0, one launch (start us, length us, event | category | flops | bytes accessed | tf_op | source)
XLA Modules:
  0.0 112.5 jit_solution(1476737656934812742)
XLA Ops:
  0.6 0.7 convert_multiply_fusion.1
  1.3 0.1 broadcast_in_dim.10
  1.4 0.1 reshape.9
  1.4 0.1 pad.2.clone
  1.5 0.7 convert_multiply_fusion
  2.3 0.8 maximum_maximum_fusion.observed_in
  3.1 106.4 %analysis.1 = (f32[80,32,128]{2,1,0:T(8,128)S(1)}, f32[80,32,128]{2,1,0:T(8,128)S(1)}, f32[80,32,128]{2,1,0:T(8,128)S(1)}, f32[3,32,128]{2,1,0:T(8,128)S(1)}) custom-call(f32[80,32,128]{2,1,0:T(8,128)} %h_in.1, f32[80,32,128]{2,1,0:T(8,128)} %u_in.1, f32[80,32,128]{2,1,0:T(8,128)} %v_in.1, f32[80,128]{1,0:T(8,128)S(1)} %maximum_maximum_fusion.observed_in), custom_call_target="tpu_custom_call" | custom-call | tf_op jit(solution)/shard_map/analysis/pallas_call | solution.py:619
  109.5 1.2 %broadcast_add_fusion.2 = f32[80,32,128]{2,1,0:T(8,128)} fusion(f32[80,32,128]{2,1,0:T(8,128)S(1)} %get-tuple-element.7, f32[32,128]{1,0:T(8,128)S(1)} %get-tuple-element.13), kind=kLoop, calls=%fused_computation.2 | loop fusion | flops 327680 | bytes 2637824 | tf_op jit(solution)/shard_map/add | solution.py:658
  110.7 1.8 %broadcast_add_fusion = (f32[80,32,128]{2,1,0:T(8,128)}, f32[80,32,128]{2,1,0:T(8,128)}) fusion(f32[80,32,128]{2,1,0:T(8,128)S(1)} %get-tuple-element.10, f32[32,128]{1,0:T(8,128)S(1)} %get-tuple-element.11, f32[80,32,128]{2,1,0:T(8,128)S(1)} %get-tuple-element.9, f32[32,128]{1,0:T(8,128)S(1)} %get-tuple-element.12), kind=kLoop, calls=%fused_computation | loop fusion | flops 655360 | bytes 5275648 | tf_op jit(solution)/shard_map/add | solution.py:658
  (1 shorter events, 0.0 us)
